TPU v7x, 32 devices: a whole 2x2x4 slice. The times are simulated.
32 devices in a mesh: dp: 4 (over y, x), ctx: 4 (over z), tp: 2 (over core).
Axes of the slice: x: 2, y: 2, z: 4, core: 2. Of those that a mesh axis runs over, the one named last changes fastest.
Arguments:
- inputs: bfloat16 [4, 1024, 8192], P('dp', 'ctx', 'tp'), may hold values from -6 to 6
- cotangent: bfloat16 [4, 1024, 8192], P('dp', 'ctx', 'tp'), may hold values from -6 to 6
- residues: float32 [512, 16], P('tp'), may hold values from -3 to 3
- decay_rates: float32 [512, 16], P('tp'), may hold values from 0.0001953125 to 0.0333333333
- skip_gain: float32 [8192], P('tp'), may hold values from -1 to 1
Outputs:
- outputs: bfloat16 [4, 1024, 8192], P('dp', 'ctx', 'tp')
- grad_inputs: bfloat16 [4, 1024, 8192], P('dp', 'ctx', 'tp')
- grad_residues: float32 [512, 16], P('tp')
- grad_skip: float32 [8192], P('tp')
All inputs are finite; a program needn't handle non-finite values.
Results may differ from a plain program's by a relative error of at most 0.0014.
Values sent between devices are 32-bit elements; how exact they have to be, the bound alone decides.
No kernel may reach another device: no remote copies, remote signals or barrier semaphores. Data moves between devices by JAX's collectives and lax.ppermute only.
A program may use at most 128 MiB of HBM per device.

v0:
```python
import math

import jax
import jax.numpy as jnp
from jax import lax
from jax.sharding import PartitionSpec as P

highest = lax.Precision.HIGHEST


def shards(inputs, cotangent, residues, decay_rates, skip_gain):
    local_batch, block_rows, channels = inputs.shape
    group_count, mode_count = residues.shape
    group_width = channels // group_count
    sub_rows = math.gcd(256, block_rows)
    sub_count = block_rows // sub_rows
    weight = jnp.sqrt(1.0 - jnp.exp(-2.0 * decay_rates))
    coefficient = residues * weight
    positions = jnp.arange(sub_rows, dtype=jnp.float32)
    center = (sub_rows - 1) / 2.0
    rate_cube = decay_rates[:, :, None]
    decay_down = jnp.exp(-rate_cube * (positions - center))
    decay_up = jnp.exp(rate_cube * (positions - center))
    from_start = jnp.exp(-rate_cube * positions)
    to_end = jnp.exp(-rate_cube * (sub_rows - 1.0 - positions))
    five_shape = (local_batch, sub_count, sub_rows, group_count, group_width)
    state_shape = (local_batch, mode_count, channels)
    state_split = (local_batch, mode_count, group_count, group_width)
    inputs_wide = inputs.astype(jnp.float32).reshape(five_shape)
    cotangent_wide = cotangent.astype(jnp.float32).reshape(five_shape)
    sub_ends = jnp.einsum("gmt,bktgc->kbmgc", to_end, inputs_wide, precision=highest)
    sub_starts = jnp.einsum("gmt,bktgc->kbmgc", from_start, cotangent_wide, precision=highest)
    device_end = sub_ends[0]
    device_start = sub_starts[sub_count - 1]
    end_states = device_end.reshape(state_shape)
    start_states = device_start.reshape(state_shape)
    channel_rates = jnp.repeat(decay_rates.T, group_width, axis=1) * float(block_rows)
    gathered_x, gathered_d = (
        lax.all_gather(end_states[None], "ctx", axis=0, tiled=True),
        lax.all_gather(start_states[None], "ctx", axis=0, tiled=True),
    )
    shard_count = gathered_x.shape[0]
    position = lax.axis_index("ctx")
    others = jnp.arange(shard_count, dtype=jnp.int32)
    gap_before = jnp.maximum(position - 1 - others, 0).astype(jnp.float32)
    gap_after = jnp.maximum(others - position - 1, 0).astype(jnp.float32)
    weights_before = jnp.where(
        (others < position)[:, None, None],
        jnp.exp(-channel_rates[None] * gap_before[:, None, None]),
        0.0,
    )
    weights_after = jnp.where(
        (others > position)[:, None, None],
        jnp.exp(-channel_rates[None] * gap_after[:, None, None]),
        0.0,
    )
    state_before = jnp.sum(weights_before[:, None] * gathered_x, axis=0)
    state_after = jnp.sum(weights_after[:, None] * gathered_d, axis=0)
    block_count = math.gcd(group_count, 16)
    per_block = group_count // block_count
    causal_mask = positions[:, None] >= positions[None, :]

    def by_groups(array):
        return array.reshape((block_count, per_block) + array.shape[1:])

    def data_blocks(array):
        return array.reshape(
            local_batch, sub_count, sub_rows, block_count, per_block, group_width
        ).transpose(3, 0, 1, 2, 4, 5)

    def local_block(pieces):
        coef_piece, down_piece, up_piece, weight_piece, wide_x, wide_d, half_x, half_d = pieces
        kernel = jnp.where(
            causal_mask,
            jnp.einsum("gm,gmt,gms->gts", coef_piece, down_piece, up_piece, precision=highest),
            0.0,
        )
        local_out = jnp.einsum("gts,bksgc->bktgc", kernel, wide_x, precision=highest)
        local_back = jnp.einsum("gts,bktgc->bksgc", kernel, wide_d, precision=highest)
        pairs = jnp.einsum("bktgc,bksgc->gts", half_d, half_x, preferred_element_type=jnp.float32)
        pairs = jnp.where(causal_mask, pairs, 0.0)
        local_grad = weight_piece * jnp.einsum(
            "gmt,gts,gms->gm", down_piece, pairs, up_piece, precision=highest
        )
        return (local_out, local_back, local_grad)

    half_inputs = inputs.reshape(five_shape)
    half_cotangent = cotangent.reshape(five_shape)
    block_out, block_back, block_grad = lax.map(
        local_block,
        (
            by_groups(coefficient),
            by_groups(decay_down),
            by_groups(decay_up),
            by_groups(weight),
            data_blocks(inputs_wide),
            data_blocks(cotangent_wide),
            data_blocks(half_inputs),
            data_blocks(half_cotangent),
        ),
    )
    local_out = block_out.transpose(1, 2, 3, 0, 4, 5).reshape(five_shape)
    local_back = block_back.transpose(1, 2, 3, 0, 4, 5).reshape(five_shape)
    local_grad = block_grad.reshape(group_count, mode_count)
    running = state_before.reshape(state_split)
    before_list = [running]
    running = state_after.reshape(state_split)
    after_list = [None] * sub_count
    after_list[0] = running
    before_stack = jnp.stack(before_list, axis=1)
    after_stack = jnp.stack(after_list, axis=1)
    first_weights = coefficient[:, :, None] * jnp.exp(-rate_cube * (positions + 1.0))
    last_weights = coefficient[:, :, None] * jnp.exp(-rate_cube * (sub_rows - positions))
    carried_out = jnp.einsum("gmt,bkmgc->bktgc", first_weights, before_stack, precision=highest)
    carried_back = jnp.einsum("gmt,bkmgc->bktgc", last_weights, after_stack, precision=highest)
    carried_grad = (
        weight
        * jnp.exp(-decay_rates)
        * jnp.einsum("kbmgc,bkmgc->gm", sub_starts, before_stack, precision=highest)
    )
    skip_wide = skip_gain.reshape(group_count, group_width)
    outputs = (
        (local_out + carried_out + skip_wide * inputs_wide)
        .reshape(local_batch, block_rows, channels)
        .astype(jnp.bfloat16)
    )
    grad_inputs = (
        (local_back + carried_back + skip_wide * cotangent_wide)
        .reshape(local_batch, block_rows, channels)
        .astype(jnp.bfloat16)
    )
    token_total = local_batch * block_rows * lax.axis_size("dp") * lax.axis_size("ctx")
    scale = 1.0 / math.sqrt(token_total)
    skip_local = jnp.sum(inputs_wide * cotangent_wide, axis=(0, 1, 2)).reshape(channels)
    grad_residues, grad_skip = lax.psum(
        ((local_grad + carried_grad) * scale, skip_local * scale), ("dp", "ctx")
    )
    return (outputs, grad_inputs, grad_residues, grad_skip)


def solution(mesh):
    placed = (P("dp", "ctx", "tp"), P("dp", "ctx", "tp"), P("tp", None), P("tp", None), P("tp"))
    return jax.shard_map(
        shards,
        mesh=mesh,
        in_specs=placed,
        out_specs=(P("dp", "ctx", "tp"), P("dp", "ctx", "tp"), P("tp", None), P("tp")),
        check_vma=False,
    )
```

profile of v0, /device:TPU:0, one launch (start us, length us, event | category | flops | bytes accessed | tf_op | source)
XLA Modules:
  0.0 482.6 jit_solution(7826191395345889366)
XLA Ops:
  38.0 4.3 copy.69
  46.3 309.6 %while.16 = (s32[]{:T(128)}, f32[16,1,1,256,16,16]{3,5,4,2,1,0:T(8,128)}, f32[16,1,1,256,16,16]{3,5,4,2,1,0:T(8,128)}, f32[16,16,16]{2,1,0:T(8,128)S(1)}, f32[16...) while((s32[]{:T(128)}, ...), condition=%wide.region_1.2_spmd.clone.clone, body=%wide.region_0.1_spmd.clone.clone.sunk | while | flops 842268672 | bytes 23626892 | solution.py:89
  46.3 4.7 fusion.124
  51.1 5.2 %fusion.125 = f32[16,1,1,256,16,16]{3,5,4,2,1,0:T(8,128)} fusion(f32[16,1,1,256,16,16]{3,5,4,2,1,0:T(8,128)} %get-tuple-element.324, s32[]{:T(128)S(6)} %copy.116, f32[16,256,256]{2,1,0:T(8,128)S(1)} %fusion.124, pred[256,256]{1,0:T(8,128)(4,1)S(1)} %iota_compare_fusion.4, f32[16,1,1,256,16,16]{3,5,4,2,1,0:T(8,128)} %get-tuple-element.340), kind=kOutput, calls=%fused_computation.14.clone.1 | convolution fusion | flops 202375168 | bytes 4785152 | tf_op jit(solution)/shard_map/while/body/eval_jaxpr/gts,bksgc->bktgc/dot_general | solution.py:78
  65.7 4.7 fusion.124
  70.5 5.2 %fusion.125 = f32[16,1,1,256,16,16]{3,5,4,2,1,0:T(8,128)} fusion(f32[16,1,1,256,16,16]{3,5,4,2,1,0:T(8,128)} %get-tuple-element.324, s32[]{:T(128)S(6)} %copy.116, f32[16,256,256]{2,1,0:T(8,128)S(1)} %fusion.124, pred[256,256]{1,0:T(8,128)(4,1)S(1)} %iota_compare_fusion.4, f32[16,1,1,256,16,16]{3,5,4,2,1,0:T(8,128)} %get-tuple-element.340), kind=kOutput, calls=%fused_computation.14.clone.1 | convolution fusion | flops 202375168 | bytes 4785152 | tf_op jit(solution)/shard_map/while/body/eval_jaxpr/gts,bksgc->bktgc/dot_general | solution.py:78
  85.0 4.7 fusion.124
  89.8 5.2 %fusion.125 = f32[16,1,1,256,16,16]{3,5,4,2,1,0:T(8,128)} fusion(f32[16,1,1,256,16,16]{3,5,4,2,1,0:T(8,128)} %get-tuple-element.324, s32[]{:T(128)S(6)} %copy.116, f32[16,256,256]{2,1,0:T(8,128)S(1)} %fusion.124, pred[256,256]{1,0:T(8,128)(4,1)S(1)} %iota_compare_fusion.4, f32[16,1,1,256,16,16]{3,5,4,2,1,0:T(8,128)} %get-tuple-element.340), kind=kOutput, calls=%fused_computation.14.clone.1 | convolution fusion | flops 202375168 | bytes 4785152 | tf_op jit(solution)/shard_map/while/body/eval_jaxpr/gts,bksgc->bktgc/dot_general | solution.py:78
  104.3 4.7 fusion.124
  109.1 5.2 %fusion.125 = f32[16,1,1,256,16,16]{3,5,4,2,1,0:T(8,128)} fusion(f32[16,1,1,256,16,16]{3,5,4,2,1,0:T(8,128)} %get-tuple-element.324, s32[]{:T(128)S(6)} %copy.116, f32[16,256,256]{2,1,0:T(8,128)S(1)} %fusion.124, pred[256,256]{1,0:T(8,128)(4,1)S(1)} %iota_compare_fusion.4, f32[16,1,1,256,16,16]{3,5,4,2,1,0:T(8,128)} %get-tuple-element.340), kind=kOutput, calls=%fused_computation.14.clone.1 | convolution fusion | flops 202375168 | bytes 4785152 | tf_op jit(solution)/shard_map/while/body/eval_jaxpr/gts,bksgc->bktgc/dot_general | solution.py:78
  123.7 4.7 fusion.124
  128.4 5.3 %fusion.125 = f32[16,1,1,256,16,16]{3,5,4,2,1,0:T(8,128)} fusion(f32[16,1,1,256,16,16]{3,5,4,2,1,0:T(8,128)} %get-tuple-element.324, s32[]{:T(128)S(6)} %copy.116, f32[16,256,256]{2,1,0:T(8,128)S(1)} %fusion.124, pred[256,256]{1,0:T(8,128)(4,1)S(1)} %iota_compare_fusion.4, f32[16,1,1,256,16,16]{3,5,4,2,1,0:T(8,128)} %get-tuple-element.340), kind=kOutput, calls=%fused_computation.14.clone.1 | convolution fusion | flops 202375168 | bytes 4785152 | tf_op jit(solution)/shard_map/while/body/eval_jaxpr/gts,bksgc->bktgc/dot_general | solution.py:78
  133.7 4.0 fusion.126
  143.0 4.7 fusion.124
  147.8 5.3 %fusion.125 = f32[16,1,1,256,16,16]{3,5,4,2,1,0:T(8,128)} fusion(f32[16,1,1,256,16,16]{3,5,4,2,1,0:T(8,128)} %get-tuple-element.324, s32[]{:T(128)S(6)} %copy.116, f32[16,256,256]{2,1,0:T(8,128)S(1)} %fusion.124, pred[256,256]{1,0:T(8,128)(4,1)S(1)} %iota_compare_fusion.4, f32[16,1,1,256,16,16]{3,5,4,2,1,0:T(8,128)} %get-tuple-element.340), kind=kOutput, calls=%fused_computation.14.clone.1 | convolution fusion | flops 202375168 | bytes 4785152 | tf_op jit(solution)/shard_map/while/body/eval_jaxpr/gts,bksgc->bktgc/dot_general | solution.py:78
  153.1 4.0 fusion.126
  162.4 4.7 fusion.124
  167.2 5.2 %fusion.125 = f32[16,1,1,256,16,16]{3,5,4,2,1,0:T(8,128)} fusion(f32[16,1,1,256,16,16]{3,5,4,2,1,0:T(8,128)} %get-tuple-element.324, s32[]{:T(128)S(6)} %copy.116, f32[16,256,256]{2,1,0:T(8,128)S(1)} %fusion.124, pred[256,256]{1,0:T(8,128)(4,1)S(1)} %iota_compare_fusion.4, f32[16,1,1,256,16,16]{3,5,4,2,1,0:T(8,128)} %get-tuple-element.340), kind=kOutput, calls=%fused_computation.14.clone.1 | convolution fusion | flops 202375168 | bytes 4785152 | tf_op jit(solution)/shard_map/while/body/eval_jaxpr/gts,bksgc->bktgc/dot_general | solution.py:78
  172.4 4.0 fusion.126
  181.7 4.7 fusion.124
  186.5 5.2 %fusion.125 = f32[16,1,1,256,16,16]{3,5,4,2,1,0:T(8,128)} fusion(f32[16,1,1,256,16,16]{3,5,4,2,1,0:T(8,128)} %get-tuple-element.324, s32[]{:T(128)S(6)} %copy.116, f32[16,256,256]{2,1,0:T(8,128)S(1)} %fusion.124, pred[256,256]{1,0:T(8,128)(4,1)S(1)} %iota_compare_fusion.4, f32[16,1,1,256,16,16]{3,5,4,2,1,0:T(8,128)} %get-tuple-element.340), kind=kOutput, calls=%fused_computation.14.clone.1 | convolution fusion | flops 202375168 | bytes 4785152 | tf_op jit(solution)/shard_map/while/body/eval_jaxpr/gts,bksgc->bktgc/dot_general | solution.py:78
  191.8 4.0 fusion.126
  201.1 4.7 fusion.124
  205.8 5.3 %fusion.125 = f32[16,1,1,256,16,16]{3,5,4,2,1,0:T(8,128)} fusion(f32[16,1,1,256,16,16]{3,5,4,2,1,0:T(8,128)} %get-tuple-element.324, s32[]{:T(128)S(6)} %copy.116, f32[16,256,256]{2,1,0:T(8,128)S(1)} %fusion.124, pred[256,256]{1,0:T(8,128)(4,1)S(1)} %iota_compare_fusion.4, f32[16,1,1,256,16,16]{3,5,4,2,1,0:T(8,128)} %get-tuple-element.340), kind=kOutput, calls=%fused_computation.14.clone.1 | convolution fusion | flops 202375168 | bytes 4785152 | tf_op jit(solution)/shard_map/while/body/eval_jaxpr/gts,bksgc->bktgc/dot_general | solution.py:78
  211.1 4.0 fusion.126
  220.4 4.7 fusion.124
  225.2 5.2 %fusion.125 = f32[16,1,1,256,16,16]{3,5,4,2,1,0:T(8,128)} fusion(f32[16,1,1,256,16,16]{3,5,4,2,1,0:T(8,128)} %get-tuple-element.324, s32[]{:T(128)S(6)} %copy.116, f32[16,256,256]{2,1,0:T(8,128)S(1)} %fusion.124, pred[256,256]{1,0:T(8,128)(4,1)S(1)} %iota_compare_fusion.4, f32[16,1,1,256,16,16]{3,5,4,2,1,0:T(8,128)} %get-tuple-element.340), kind=kOutput, calls=%fused_computation.14.clone.1 | convolution fusion | flops 202375168 | bytes 4785152 | tf_op jit(solution)/shard_map/while/body/eval_jaxpr/gts,bksgc->bktgc/dot_general | solution.py:78
  230.4 4.0 fusion.126
  239.8 4.7 fusion.124
  244.5 5.3 %fusion.125 = f32[16,1,1,256,16,16]{3,5,4,2,1,0:T(8,128)} fusion(f32[16,1,1,256,16,16]{3,5,4,2,1,0:T(8,128)} %get-tuple-element.324, s32[]{:T(128)S(6)} %copy.116, f32[16,256,256]{2,1,0:T(8,128)S(1)} %fusion.124, pred[256,256]{1,0:T(8,128)(4,1)S(1)} %iota_compare_fusion.4, f32[16,1,1,256,16,16]{3,5,4,2,1,0:T(8,128)} %get-tuple-element.340), kind=kOutput, calls=%fused_computation.14.clone.1 | convolution fusion | flops 202375168 | bytes 4785152 | tf_op jit(solution)/shard_map/while/body/eval_jaxpr/gts,bksgc->bktgc/dot_general | solution.py:78
  249.8 4.0 fusion.126
  259.1 4.7 fusion.124
  263.9 5.3 %fusion.125 = f32[16,1,1,256,16,16]{3,5,4,2,1,0:T(8,128)} fusion(f32[16,1,1,256,16,16]{3,5,4,2,1,0:T(8,128)} %get-tuple-element.324, s32[]{:T(128)S(6)} %copy.116, f32[16,256,256]{2,1,0:T(8,128)S(1)} %fusion.124, pred[256,256]{1,0:T(8,128)(4,1)S(1)} %iota_compare_fusion.4, f32[16,1,1,256,16,16]{3,5,4,2,1,0:T(8,128)} %get-tuple-element.340), kind=kOutput, calls=%fused_computation.14.clone.1 | convolution fusion | flops 202375168 | bytes 4785152 | tf_op jit(solution)/shard_map/while/body/eval_jaxpr/gts,bksgc->bktgc/dot_general | solution.py:78
  269.2 4.0 fusion.126
  278.5 4.7 fusion.124
  283.3 5.2 %fusion.125 = f32[16,1,1,256,16,16]{3,5,4,2,1,0:T(8,128)} fusion(f32[16,1,1,256,16,16]{3,5,4,2,1,0:T(8,128)} %get-tuple-element.324, s32[]{:T(128)S(6)} %copy.116, f32[16,256,256]{2,1,0:T(8,128)S(1)} %fusion.124, pred[256,256]{1,0:T(8,128)(4,1)S(1)} %iota_compare_fusion.4, f32[16,1,1,256,16,16]{3,5,4,2,1,0:T(8,128)} %get-tuple-element.340), kind=kOutput, calls=%fused_computation.14.clone.1 | convolution fusion | flops 202375168 | bytes 4785152 | tf_op jit(solution)/shard_map/while/body/eval_jaxpr/gts,bksgc->bktgc/dot_general | solution.py:78
  297.8 4.7 fusion.124
  302.6 5.2 %fusion.125 = f32[16,1,1,256,16,16]{3,5,4,2,1,0:T(8,128)} fusion(f32[16,1,1,256,16,16]{3,5,4,2,1,0:T(8,128)} %get-tuple-element.324, s32[]{:T(128)S(6)} %copy.116, f32[16,256,256]{2,1,0:T(8,128)S(1)} %fusion.124, pred[256,256]{1,0:T(8,128)(4,1)S(1)} %iota_compare_fusion.4, f32[16,1,1,256,16,16]{3,5,4,2,1,0:T(8,128)} %get-tuple-element.340), kind=kOutput, calls=%fused_computation.14.clone.1 | convolution fusion | flops 202375168 | bytes 4785152 | tf_op jit(solution)/shard_map/while/body/eval_jaxpr/gts,bksgc->bktgc/dot_general | solution.py:78
  317.1 4.7 fusion.124
  321.9 5.2 %fusion.125 = f32[16,1,1,256,16,16]{3,5,4,2,1,0:T(8,128)} fusion(f32[16,1,1,256,16,16]{3,5,4,2,1,0:T(8,128)} %get-tuple-element.324, s32[]{:T(128)S(6)} %copy.116, f32[16,256,256]{2,1,0:T(8,128)S(1)} %fusion.124, pred[256,256]{1,0:T(8,128)(4,1)S(1)} %iota_compare_fusion.4, f32[16,1,1,256,16,16]{3,5,4,2,1,0:T(8,128)} %get-tuple-element.340), kind=kOutput, calls=%fused_computation.14.clone.1 | convolution fusion | flops 202375168 | bytes 4785152 | tf_op jit(solution)/shard_map/while/body/eval_jaxpr/gts,bksgc->bktgc/dot_general | solution.py:78
  336.5 4.7 fusion.124
  341.2 5.2 %fusion.125 = f32[16,1,1,256,16,16]{3,5,4,2,1,0:T(8,128)} fusion(f32[16,1,1,256,16,16]{3,5,4,2,1,0:T(8,128)} %get-tuple-element.324, s32[]{:T(128)S(6)} %copy.116, f32[16,256,256]{2,1,0:T(8,128)S(1)} %fusion.124, pred[256,256]{1,0:T(8,128)(4,1)S(1)} %iota_compare_fusion.4, f32[16,1,1,256,16,16]{3,5,4,2,1,0:T(8,128)} %get-tuple-element.340), kind=kOutput, calls=%fused_computation.14.clone.1 | convolution fusion | flops 202375168 | bytes 4785152 | tf_op jit(solution)/shard_map/while/body/eval_jaxpr/gts,bksgc->bktgc/dot_general | solution.py:78
  346.5 4.0 fusion.126
  369.3 10.1 %fusion.62 = bf16[1,1,256,256,16]{2,4,3,1,0:T(8,128)(2,1)} fusion(f32[1,1,256,256,16]{2,4,3,1,0:T(8,128)} %bitcast.159, f32[1,1,256,256,16]{2,4,3,1,0:T(8,128)S(1)} %bitcast.154, f32[256,16]{1,0:T(8,128)S(1)} %mul.240, f32[256]{0:T(256)S(1)} %iota_add_fusion, f32[256,16]{1,0:T(8,128)S(1)} %bitcast.167, f32[256,16]{1,0:T(8,128)S(1)} %copy.99, ...), kind=kOutput, calls=%fused_computation.54 | convolution fusion | flops 207618048 | bytes 10798080 | tf_op jit(solution)/shard_map/gmt,bkmgc->bktgc/dot_general | solution.py:114
  379.4 4.1 copy.85
  384.1 8.1 %fusion.60 = bf16[1,1,256,256,16]{2,4,3,1,0:T(8,128)(2,1)} fusion(f32[1,1,256,256,16]{2,4,3,1,0:T(8,128)} %bitcast.160, f32[1,1,256,256,16]{2,4,3,1,0:T(8,128)} %bitcast.152, f32[256,16]{1,0:T(8,128)S(1)} %mul.240, f32[16,256,16]{0,2,1:T(8,128)S(1)} %bitcast.155, f32[256]{0:T(256)S(1)} %iota_subtract_fusion, f32[256,16]{1,0:T(8,128)S(1)} %bitcast.168, ...), kind=kOutput, calls=%fused_computation.51 | convolution fusion | flops 207618048 | bytes 10798080 | tf_op jit(solution)/shard_map/gmt,bkmgc->bktgc/dot_general | solution.py:115
  392.2 4.1 copy.86
  396.3 79.5 %all-reduce = (f32[256,16]{0,1:T(8,128)}, f32[4096]{0:T(1024)}) all-reduce(f32[256,16]{0,1:T(8,128)S(1)} %add_multiply_fusion, f32[4096]{0:T(1024)S(1)} %broadcast_multiply_fusion), channel_id=1, replica_groups=mesh['dp'=4,'ctx'=4,'tp'=2] {'dp','ctx'}, use_global_device_ids=true, to_apply=%region_4.5 | all-reduce | flops 8192 | bytes 65536 | tf_op jit(solution)/shard_map/psum | solution.py:135
  (140 shorter events, 162.6 us)
Async XLA Ops:
  7.2 356.4 %all-gather.5.cloned.1.call-start = ((), (), s32[]{:S(2)}) async-start(), calls=%async_computation.1 | async-start | bytes 1310720 | tf_op jit(solution)/shard_map/all_gather | solution.py:40
  11.3 1.3 copy-start.3
  15.3 1.4 copy-start.2
  15.3 7.3 %copy-start.1 = (bf16[1,256,4096]{2,1,0:T(8,128)(2,1)S(1)}, bf16[1,256,4096]{2,1,0:T(8,128)(2,1)}, u32[]{:S(2)}) copy-start(bf16[1,256,4096]{2,1,0:T(8,128)(2,1)} %param.7) | copy-start | bytes 6291460
  22.6 341.1 %all-gather.3.cloned.1.call-start = ((), (), s32[]{:S(2)}) async-start(), calls=%async_computation | async-start | bytes 1310720 | tf_op jit(solution)/shard_map/all_gather | solution.py:39
  30.9 6.9 %copy-start.4 = (f32[256,16]{0,1:T(8,128)S(1)}, f32[256,16]{0,1:T(8,128)}, u32[]{:S(2)}) copy-start(f32[256,16]{0,1:T(8,128)} %param.10) | copy-start | bytes 49156
  46.3 309.7 %copy-start.5 = (f32[4096]{0:T(1024)S(1)}, f32[4096]{0:T(1024)}, u32[]{:S(2)}) copy-start(f32[4096]{0:T(1024)} %param.11) | copy-start | bytes 49156
  366.4 2.9 copy-start
Sparse Core Ops, SparseCore 0:
  22.7 30.6 all-gather.4
  55.0 27.3 all-gather.2
where the time goes:
time: 485 us; the launch traced here: 483 us
  matrix products  332 us (68%)
  blocking collectives  79.5 us (16%)
  local copies, waits for them, and re-layouts  42.6 us (9%)
  between operations  14.3 us (3%)
  other arithmetic  13.1 us (3%)
    dot_general x16, matrix products, local_block(): jnp.einsum('gts,bksgc->bktgc', kernel, wide_x, precision=highest)  83.8 us
    psum x1, blocking collectives, shards(): lax.psum(((local_grad + carried_grad) * scale, skip_local * scale), ('dp'...  79.5 us
    dot_general x16, matrix products, local_block(): jnp.einsum('gm,gmt,gms->gts', coef_piece, down_piece, up_piece, precision...  75.3 us
    dot_general x16, matrix products, local_block(): jnp.einsum('gts,bktgc->bksgc', kernel, wide_d, precision=highest)  63.3 us
    dot_general x16, matrix products, local_block(): jnp.einsum('gmt,gts,gms->gm', down_piece, pairs, up_piece, precision=high...  57.7 us
    dot_general x16, matrix products, local_block(): jnp.einsum('bktgc,bksgc->gts', half_d, half_x, preferred_element_type=jnp...  27.4 us
    unnamed x18, local copies, waits for them, and re-layouts  16.7 us
    dot_general x1, matrix products, shards(): jnp.einsum('gmt,bkmgc->bktgc', first_weights, before_stack, precision=hig...  10.1 us
  transfers between devices with their start and end apart: 2, of which 0 were waited for; matrix products, arithmetic and copies ran while one was open for 70% of the time, Pallas kernels for 0%

commit v1 on v0

v1 whole, which is shorter than its diff:
```python
import functools
import math

import jax
import jax.numpy as jnp
from jax import lax
from jax.experimental import pallas as pl
from jax.experimental.pallas import tpu as pltpu
from jax.sharding import PartitionSpec as P


f32 = jnp.float32
bf16 = jnp.bfloat16
LANES = 128
TILES_A, TILES_B, TILES_C = 8, 2, 8
VMEM_LIMIT = 24 * 2**20
CUTS = (6, 11)


def split(value):
    high = value.astype(bf16)
    low = (value - high.astype(f32)).astype(bf16)
    return high, low


def mm(left, right):
    return lax.dot_general(left, right, (((1,), (0,)), ((), ())), preferred_element_type=f32)


def iota(shape, axis):
    return lax.broadcasted_iota(jnp.int32, shape, axis)


def sel_rows(full, block, owner):
    total = full[0:block]
    for g in range(1, full.shape[0] // block):
        total = jnp.where(owner == g, full[g * block : (g + 1) * block], total)
    return total


def stack(parts, axis):
    return jnp.concatenate(parts, axis=axis)


def column(row, eye):
    return jnp.sum(jnp.where(eye, row, 0.0), axis=1, keepdims=True)


def ends_kernel(width, modes, tiles, x_ref, d_ref, rate_ref, near_ref, far_ref, wide_ref):
    rows = x_ref.shape[0]
    sq = (LANES, LANES)
    eye = iota(sq, 0) == iota(sq, 1)
    same = (iota(sq, 0) // width == iota(sq, 1) // width).astype(bf16)
    owner = iota((modes, LANES), 1) // width
    pick = iota((modes, LANES), 0) == iota((modes, LANES), 1) % width
    spot = iota(sq, 1).astype(f32)
    even = lax.axis_index("ctx") % 2 == 0
    pieces = rows // LANES
    for k in range(tiles):
        lanes = slice(k * LANES, (k + 1) * LANES)
        row = rate_ref[:, lanes]
        rate = column(row, eye)
        spread = jnp.where(pick, row, 0.0)
        a = spread.astype(bf16)
        b = (spread - a.astype(f32)).astype(bf16)
        c = (spread - a.astype(f32) - b.astype(f32)).astype(bf16)
        rate_wide = mm(a, same) + mm(b, same) + mm(c, same)
        wide_ref[:, lanes] = rate_wide
        step = jnp.exp(-rate_wide * float(LANES))
        got = []
        for power, src in ((LANES - 1.0 - spot, x_ref), (spot, d_ref)):
            high, low = split(jnp.exp(-rate * power))
            flat = stack([src[h * LANES : (h + 1) * LANES, lanes] for h in range(pieces)], 1)
            full = mm(stack([high, low], 1), stack([flat, flat], 0))
            got.append([sel_rows(full[:, h * LANES : (h + 1) * LANES], modes, owner) for h in range(pieces)])
        end = got[0][0]
        for h in range(1, pieces):
            end = end * step + got[0][h]
        start = got[1][pieces - 1]
        for h in range(pieces - 2, -1, -1):
            start = start * step + got[1][h]
        near_ref[:, lanes] = jnp.where(even, end, start)
        far_ref[:, lanes] = jnp.where(even, start, end)


def local_kernel(width, modes, tiles, *refs):
    x_ref, d_ref, rate_ref, wide_ref, coef_ref, skip_ref = refs[:6]
    yx_ref, yd_ref, grad_ref, far_ref, gskip_ref, own_ref = refs[-6:]
    rows = x_ref.shape[0]
    groups = LANES // width
    fold = max(1, 2 * LANES // (groups * modes))
    chunk = fold * modes
    count = rows // chunk
    sq = (LANES, LANES)

    @pl.when(pl.program_id(0) == 0)
    def _():
        own_ref[...] = ((iota(sq, 0) // modes) == (iota(sq, 1) // width)).astype(bf16)

    own = own_ref[...]
    owner = iota((chunk, LANES), 1) // width
    flat = (chunk, fold * LANES)
    t_int = iota(flat, 0)
    s_int = iota(flat, 1) // LANES * modes + iota(flat, 1) % modes
    spot = iota((chunk, LANES), 0).astype(f32)
    place = iota((modes, LANES), 1) % modes

    def spread(compact):
        return stack([compact] * groups, 0) * own

    def tall(compact):
        return stack([spread(compact[f * modes : (f + 1) * modes]) for f in range(fold)], 0)

    def broad(compact):
        return stack([spread(compact[:, f * LANES : (f + 1) * LANES]) for f in range(fold)], 1)

    def halves(value, size):
        return value[:size] + value[size:]

    def three(table_h, table_l, right_h, right_l):
        left = stack([stack([table_h, table_h], 1), stack([table_l, jnp.zeros_like(table_l)], 1)], 0)
        return halves(mm(left, stack([right_h, right_l], 0)), table_h.shape[0])

    for k in range(tiles):
        lanes = slice(k * LANES, (k + 1) * LANES)
        row, coef, wide = rate_ref[:, lanes], coef_ref[:, lanes], wide_ref[:, lanes]
        skip = skip_ref[:, lanes]
        leap = jnp.exp(-wide * float(chunk))
        down = jnp.exp(-row * spot)
        up = jnp.exp(row * spot)
        up_h, up_l = split(up)
        first_h, first_l = split(down * (coef * jnp.exp(row * (chunk - 1.0))))
        last_h, last_l = split(up * coef)
        start = stack([jnp.exp(-wide * (place + f * modes).astype(f32)) for f in range(fold)], 1)
        end = stack([jnp.exp(-wide * (chunk - 1 - f * modes - place).astype(f32)) for f in range(fold)], 1)
        start_h, start_l = split(start)
        end_h, end_l = split(end)
        forth = jnp.where(t_int >= s_int, three(first_h, first_l, broad(end_h), broad(end_l)), 0.0)
        back = jnp.where(t_int <= s_int, three(last_h, last_l, broad(start_h), broad(start_l)), 0.0)

        def tiles_of(src):
            expanded = [tall(src[j * chunk : (j + 1) * chunk, lanes]) for j in range(count)]
            return [stack(expanded[j : j + 2], 1) for j in range(0, count, 2)]

        def near_part(kernel, ends_h, ends_l, right, src, dst):
            k_h, k_l = split(kernel)
            left = stack([k_h, k_l, ends_h, ends_l], 0)
            found = []
            for p, block in enumerate(right):
                res = mm(left, block)
                own_part = halves(res[: 2 * chunk], chunk)
                ends = halves(res[2 * chunk :], modes)
                for q in range(2):
                    half = slice(q * LANES, (q + 1) * LANES)
                    spots = slice((2 * p + q) * chunk, (2 * p + q + 1) * chunk)
                    dst[spots, lanes] = own_part[:, half] + skip * src[spots, lanes].astype(f32)
                    found.append(ends[:, half])
            return found

        def far_part(table_h, table_l, states, dst):
            for p in range(0, count, 2):
                pair = [split(states[p + q]) for q in range(2)]
                res = three(
                    table_h,
                    table_l,
                    stack([spread(h) for h, _ in pair], 1),
                    stack([spread(l) for _, l in pair], 1),
                )
                for q in range(2):
                    spots = slice((p + q) * chunk, (p + q + 1) * chunk)
                    dst[spots, lanes] += res[:, q * LANES : (q + 1) * LANES]

        x_right = tiles_of(x_ref)
        ends_x = near_part(forth, end_h, end_l, x_right, x_ref, yx_ref)
        pairs = lax.dot_general(
            stack([d_ref[j * chunk : (j + 1) * chunk, lanes] for j in range(count)], 1),
            stack(x_right, 1),
            (((1,), (1,)), ((), ())),
            preferred_element_type=f32,
        )
        starts_d = near_part(back, start_h, start_l, tiles_of(d_ref), d_ref, yd_ref)
        state = jnp.zeros((modes, LANES), f32)
        states = []
        far = state
        for j in range(count):
            states.append(state)
            far = far + starts_d[j] * state
            state = (state + ends_x[j]) * leap
        far_ref[:, lanes] = far * jnp.exp(wide * float(chunk))
        far_part(first_h, first_l, states, yx_ref)
        state = jnp.zeros((modes, LANES), f32)
        states = [None] * count
        for j in range(count - 1, -1, -1):
            states[j] = state
            state = (state + starts_d[j]) * leap
        far_part(last_h, last_l, states, yd_ref)
        p_h, p_l = split(jnp.where(t_int >= s_int, pairs, 0.0))
        res = mm(stack([p_h, p_l], 0), stack([tall(up_h), tall(up_l)], 1))
        near = res[:chunk, :LANES] + res[:chunk, LANES:] + res[chunk:, :LANES]
        grad_ref[:, lanes] = jnp.sum(near * down, axis=0, keepdims=True)
        total = jnp.zeros((chunk, LANES), f32)
        for j in range(count):
            spots = slice(j * chunk, (j + 1) * chunk)
            total = total + x_ref[spots, lanes].astype(f32) * d_ref[spots, lanes].astype(f32)
        gskip_ref[:, lanes] = jnp.sum(total, axis=0, keepdims=True)


def carry_grad_kernel(width, modes, scale, four, *refs):
    out_ref = refs[-1]
    near_ref, far_ref, rate_ref, weight_ref, skip_ref = refs[:5]
    p_ref, q_ref = refs[5:7]
    sq = (LANES, LANES)
    same = ((iota(sq, 0) // width) == (iota(sq, 1) // width)).astype(bf16)
    pick = iota((modes, LANES), 0) == iota((modes, LANES), 1) % modes
    place = lax.axis_index("ctx")
    inner = ((place == 1) | (place == 2)).astype(f32)
    middle = (place == 1).astype(f32)
    for k in range(p_ref.shape[1] // LANES):
        lanes = slice(k * LANES, (k + 1) * LANES)
        value = p_ref[:, lanes] * q_ref[:, lanes]
        if four:
            r_ref, s_ref = refs[7:9]
            value = value * inner + r_ref[:, lanes] * s_ref[:, lanes] * middle
        high, low = split(value + far_ref[:, lanes])
        sums = mm(stack([high, low], 1), stack([same, same], 0))
        far = jnp.sum(jnp.where(pick, sums, 0.0), axis=0, keepdims=True)
        out_ref[0:1, lanes] = (near_ref[:, lanes] + far * jnp.exp(-rate_ref[:, lanes])) * (weight_ref[:, lanes] * scale)
        out_ref[1:2, lanes] = skip_ref[:, lanes] * scale


def finish_kernel(width, modes, tiles, forward, four, y_ref, rate_ref, wide_ref, coef_ref, *refs):
    o_ref = refs[-1]
    rows = y_ref.shape[0]
    groups = LANES // width
    sq = (LANES, LANES)
    own = ((iota(sq, 0) // modes) == (iota(sq, 1) // width)).astype(bf16)
    spot = iota((8, LANES), 0).astype(f32)
    pieces = rows // LANES
    place = lax.axis_index("ctx")
    if not forward:
        place = 3 - place
    for k in range(tiles):
        lanes = slice(k * LANES, (k + 1) * LANES)
        rate, coef, wide = rate_ref[:, lanes], coef_ref[:, lanes], wide_ref[:, lanes]
        state = refs[0][:, lanes]
        if four:
            both = state + refs[2][:, lanes] * jnp.exp(-wide * float(rows))
            state = jnp.where(place == 0, 0.0, jnp.where(place == 2, refs[1][:, lanes], both))
        step = jnp.exp(-wide * float(LANES))
        table = coef * jnp.exp(-rate * (spot + 1.0 if forward else 8.0 - spot))
        size = 8
        while size < LANES:
            more = table * jnp.exp(-rate * float(size))
            table = stack([table, more] if forward else [more, table], 0)
            size *= 2
        t_h, t_l = split(table)
        highs, lows = [], []
        for _ in range(pieces):
            s_h, s_l = split(state)
            highs.append(stack([s_h] * groups, 0) * own)
            lows.append(stack([s_l] * groups, 0) * own)
            state = state * step
        if not forward:
            highs, lows = highs[::-1], lows[::-1]
        high, low = stack(highs, 1), stack(lows, 1)
        total = mm(stack([t_h, t_l], 1), stack([high, high], 0)) + mm(t_h, low)
        for h in range(pieces):
            spots = slice(h * LANES, (h + 1) * LANES)
            o_ref[spots, lanes] = (y_ref[spots, lanes] + total[:, spots]).astype(bf16)


def swap_states(near, far, power, even, count):
    end, start = jnp.where(even, near, far), jnp.where(even, far, near)
    before, after, prior, distance = end, start, None, 1
    have_x, have_d = None, None
    while distance < count:
        got_x = lax.ppermute(before, "ctx", [(i, i + distance) for i in range(count - distance)])
        got_d = lax.ppermute(after, "ctx", [(i + distance, i) for i in range(count - distance)])
        have_x = got_x if prior is None else have_x + prior * got_x
        have_d = got_d if prior is None else have_d + prior * got_d
        prior = power if prior is None else prior * power
        before, after = before + power * got_x, after + power * got_d
        power = power * power
        distance *= 2
    return have_x, have_d, start


def layer(inputs, cotangent, residues, decay_rates, skip_gain):
    local_batch, rows, channels = inputs.shape
    group_count, modes = residues.shape
    width = channels // group_count
    x, d = inputs.reshape(local_batch * rows, channels), cotangent.reshape(local_batch * rows, channels)
    rate = decay_rates.reshape(1, channels)
    weight = jnp.sqrt(1.0 - jnp.exp(-2.0 * rate))
    coef = residues.reshape(1, channels) * weight
    skip = skip_gain.reshape(1, channels)
    count = lax.axis_size("ctx")
    four = count == 4
    blocks = channels // LANES
    every = pl.BlockSpec(memory_space=pl.ANY)
    params = pltpu.CompilerParams(vmem_limit_bytes=VMEM_LIMIT)

    def specs(tiles, offset=0):
        step = tiles * LANES
        index = lambda i: (0, i + offset)
        return pl.BlockSpec((rows, step), index), pl.BlockSpec((modes, step), index), pl.BlockSpec((1, step), index)

    tiles = math.gcd(TILES_A, blocks)
    data, state, line = specs(tiles)
    near, far, wide = pl.pallas_call(
        functools.partial(ends_kernel, width, modes, tiles),
        grid=(blocks // tiles,),
        in_specs=[data, data, line],
        out_specs=[state, state, state],
        out_shape=[jax.ShapeDtypeStruct((modes, channels), f32)] * 3,
        compiler_params=params,
        name="ends",
    )(x, d, rate)
    power = jnp.exp(-wide * float(rows))

    tiles_b = math.gcd(TILES_B, blocks)
    steps = blocks // tiles_b

    def local(first, size, past):
        data, state, line = specs(tiles_b, first)
        return pl.pallas_call(
            functools.partial(local_kernel, width, modes, tiles_b),
            grid=(size,),
            in_specs=[data, data, line, state, line, line] + ([] if past is None else [every] * 5),
            out_specs=[data, data, line, state, line],
            out_shape=[jax.ShapeDtypeStruct((rows, channels), f32)] * 2
            + [jax.ShapeDtypeStruct((size_of, channels), f32) for size_of in (1, modes, 1)],
            scratch_shapes=[pltpu.VMEM((LANES, LANES), bf16)],
            input_output_aliases={} if past is None else {6 + n: n for n in range(5)},
            compiler_params=params,
            name="local",
        )(x, d, rate, wide, coef, skip, *(past or ()))

    def swap(value, pairs):
        return lax.ppermute(value, "ctx", pairs)

    if four:
        one = swap(near, [(0, 1), (1, 0), (2, 3), (3, 2)])
        cut_a, cut_b = max(1, steps * CUTS[0] // 16), max(2, steps * CUTS[1] // 16)
        past = local(0, cut_a, None)
        meet = far + power * one
        past, meet = lax.optimization_barrier((past, meet))
        two = swap(meet, [(1, 2), (2, 1)])
        past = local(cut_a, cut_b - cut_a, past)
        past, two = lax.optimization_barrier((past, two))
        three = swap(two, [(1, 0), (2, 3)])
        y_x, y_d, grad, far_grad, gskip = local(cut_b, steps - cut_b, past)
        states_x = states_d = (one, two, three)
        factors = (one, near, meet, two)
    else:
        even = lax.axis_index("ctx") % 2 == 0
        have_x, have_d, start = swap_states(near, far, power, even, count)
        y_x, y_d, grad, far_grad, gskip = local(0, steps, None)
        states_x, states_d = (have_x,), (have_d,)
        factors = (have_x, start)

    token_total = local_batch * rows * lax.axis_size("dp") * count
    grads = pl.pallas_call(
        functools.partial(carry_grad_kernel, width, modes, 1.0 / math.sqrt(token_total), four),
        in_specs=[pl.BlockSpec(memory_space=pltpu.VMEM)] * (5 + len(factors)),
        out_shape=jax.ShapeDtypeStruct((2, channels), f32),
        compiler_params=params,
        name="carry_grad",
    )(grad, far_grad, rate, weight, gskip, *factors)

    tiles_c = math.gcd(TILES_C, blocks)
    steps = blocks // tiles_c

    def finish(forward, first, size, past):
        data, state, line = specs(tiles_c, first)
        y, states = (y_x, states_x) if forward else (y_d, states_d)
        return pl.pallas_call(
            functools.partial(finish_kernel, width, modes, tiles_c, forward, four),
            grid=(size,),
            in_specs=[data, line, state, line] + [state] * len(states) + ([] if past is None else [every]),
            out_specs=data,
            out_shape=jax.ShapeDtypeStruct((rows, channels), bf16),
            input_output_aliases={} if past is None else {4 + len(states): 0},
            compiler_params=params,
            name="finish",
        )(y, rate, wide, coef, *states, *(() if past is None else (past,)))

    results = {True: None, False: None}
    queue = [(True, 0, steps // 2), (True, steps // 2, steps - steps // 2)]
    queue += [(False, 0, steps // 2), (False, steps // 2, steps - steps // 2)]
    queue = [piece for piece in queue if piece[2] > 0]
    rounds = [("dp", k) for k in doubling(lax.axis_size("dp"))] + [("ctx", k) for k in doubling(count)]
    for axis, k in rounds:
        other = lax.ppermute(grads, axis, [(i, i ^ k) for i in range(lax.axis_size(axis))])
        if queue:
            forward, first, size = queue.pop(0)
            results[forward] = finish(forward, first, size, results[forward])
            results[forward], other = lax.optimization_barrier((results[forward], other))
        grads = grads + other
    for forward, first, size in queue:
        results[forward] = finish(forward, first, size, results[forward])
    return (
        results[True].reshape(inputs.shape),
        results[False].reshape(inputs.shape),
        grads[0].reshape(group_count, modes),
        grads[1],
    )


def doubling(size):
    return [1 << n for n in range(size.bit_length() - 1)]


def solution(mesh):
    placed = (P("dp", "ctx", "tp"), P("dp", "ctx", "tp"), P("tp", None), P("tp", None), P("tp"))
    return jax.shard_map(
        layer,
        mesh=mesh,
        in_specs=placed,
        out_specs=(P("dp", "ctx", "tp"), P("dp", "ctx", "tp"), P("tp", None), P("tp")),
        check_vma=False,
    )
```

time: 485 us -> 62.3 us (0.13)
  matrix products: 332 us -> 0 us
  blocking collectives: 79.5 us -> 0 us
  Pallas kernels: 0 us -> 37.1 us
  local copies, waits for them, and re-layouts: 42.6 us -> 7.33 us
  starting transfers between devices: 0.08 us -> 14.2 us
  between operations: 14.3 us -> 0.81 us
  other arithmetic: 13.1 us -> 0.19 us
    dot_general x84 -> x0, matrix products: 332 us -> none  [the longest x16 83.8 us: local_block(): jnp.einsum('gts,bksgc->bktgc', kernel, wide_x, precision=highest)]
    psum x1 -> x0, blocking collectives: 79.5 us -> none  [shards(): lax.psum(((local_grad + carried_grad) * scale, skip_local * scale), ('dp'...]
    pallas_call x0 -> x9, Pallas kernels: none -> 37.1 us  [the longest x3 25.6 us: local(): pl.pallas_call(functools.partial(local_kernel, width, modes, tiles_b), gr...]
    ppermute x0 -> x7, starting transfers between devices: none -> 14.2 us  [the longest x4 9.1 us: layer(): lax.ppermute(grads, axis, [(i, i ^ k) for i in range(lax.axis_size(axis))])]
    unnamed x18 -> x15, local copies, waits for them, and re-layouts: 16.7 us -> 6.38 us
    another operation x4 -> x1, local copies, waits for them, and re-layouts: 9.09 us -> 0.09 us  [layer(): grads[0].reshape(group_count, modes)]
    convert_element_type x2 -> x0, local copies, waits for them, and re-layouts: 7.24 us -> none  [the longest x1 4.3 us: shards(): cotangent_wide = cotangent.astype(jnp.float32).reshape(five_shape)]
  transfers between devices with their start and end apart: 2 -> 7, of which waited for: 0 -> 4; matrix products, arithmetic and copies ran while one was open for 70% -> 0% of each run, Pallas kernels for 0% -> 54%
where the time goes in v1:
time: 62.3 us; the launch traced here: 62 us
  Pallas kernels  37.1 us (60%)
  starting transfers between devices  14.2 us (23%)
  local copies, waits for them, and re-layouts  7.33 us (12%)
  waiting for transfers between devices  2.46 us (4%)
  between operations  0.81 us (1%)
    pallas_call x3, Pallas kernels, local(): pl.pallas_call(functools.partial(local_kernel, width, modes, tiles_b), gr...  25.6 us
    ppermute x4, starting transfers between devices, layer(): lax.ppermute(grads, axis, [(i, i ^ k) for i in range(lax.axis_size(axis))])  9.1 us
    pallas_call x4, Pallas kernels, finish(): pl.pallas_call(functools.partial(finish_kernel, width, modes, tiles_c, fo...  7.7 us
    unnamed x15, local copies, waits for them, and re-layouts  6.38 us
    ppermute x3, starting transfers between devices, swap(): return lax.ppermute(value, 'ctx', pairs)  5.09 us
    pallas_call x1, Pallas kernels, layer(): pl.pallas_call(functools.partial(ends_kernel, width, modes, tiles), grid=...  3.37 us
    ppermute x4, waiting for transfers between devices, layer(): lax.ppermute(grads, axis, [(i, i ^ k) for i in range(lax.axis_size(axis))])  2.33 us
  transfers between devices with their start and end apart: 7, of which 4 were waited for; matrix products, arithmetic and copies ran while one was open for 0% of the time, Pallas kernels for 54%

profile of v1, /device:TPU:0, one launch (start us, length us, event | category | flops | bytes accessed | tf_op | source)
XLA Modules:
  0.0 62.0 jit_solution(9756666383157770128)
XLA Ops:
  0.6 0.0 copy-start.5
  0.6 0.0 copy-start.4
  0.7 0.8 %copy.24 = f32[256,16]{1,0:T(8,128)S(1)} copy(f32[256,16]{0,1:T(8,128)} %param.8) | data formatting | bytes 32768 | tf_op args[3]
  1.5 0.1 reshape.71.rate_ref.refs_2_
  1.6 0.0 copy-start
  1.6 1.6 %copy-done = bf16[1,256,4096]{2,1,0:T(8,128)(2,1)S(1)} copy-done((bf16[1,256,4096]{2,1,0:T(8,128)(2,1)S(1)}, bf16[1,256,4096]{2,1,0:T(8,128)(2,1)}, u32[]{:S(2)}) %copy-start) | copy-done | bytes 2097176
  3.2 0.0 copy-start.2
  3.2 1.6 %copy-done.2 = bf16[1,256,4096]{2,1,0:T(8,128)(2,1)S(1)} copy-done((bf16[1,256,4096]{2,1,0:T(8,128)(2,1)S(1)}, bf16[1,256,4096]{2,1,0:T(8,128)(2,1)}, u32[]{:S(2)}) %copy-start.2) | copy-done | bytes 2097176
  4.8 0.0 copy-start.1
  4.8 3.4 %ends.1 = (f32[16,4096]{1,0:T(8,128)S(1)}, f32[16,4096]{1,0:T(8,128)S(1)}, f32[16,4096]{1,0:T(8,128)S(1)}) custom-call(bf16[256,4096]{1,0:T(8,128)(2,1)S(1)} %bitcast.6, bf16[256,4096]{1,0:T(8,128)(2,1)S(1)} %bitcast.10, f32[1,4096]{1,0:T(1,128)S(1)} %reshape.71.rate_ref.refs_2_), custom_call_target="tpu_custom_call" | custom-call | tf_op jit(solution)/shard_map/ends/pallas_call | solution.py:310
  8.2 3.1 %collective-permute-start = (f32[16,4096]{1,0:T(8,128)S(1)}, f32[16,4096]{1,0:T(8,128)S(1)}, u32[]{:S(2)}, u32[]{:S(2)}) collective-permute-start(f32[16,4096]{1,0:T(8,128)S(1)} %get-tuple-element.49.refs_6_), channel_id=1, source_target_pairs={{0,2},{2,0},{4,6},{6,4},{1,3},{3,1},{5,7},{7,5},{8,10},{10,8},{12,... | collective-permute-start | bytes 786440 | tf_op jit(solution)/shard_map/ppermute | solution.py:340
  11.3 0.0 copy-done.5
  11.3 0.1 copy.25
  11.4 0.1 reshape.72
  11.5 0.1 fusion
  11.6 0.0 copy-done.4
  11.6 0.0 copy-done.1
  11.6 0.0 copy-start.3
  11.6 1.6 %copy-done.3 = bf16[1,256,4096]{2,1,0:T(8,128)(2,1)S(1)} copy-done((bf16[1,256,4096]{2,1,0:T(8,128)(2,1)S(1)}, bf16[1,256,4096]{2,1,0:T(8,128)(2,1)}, u32[]{:S(2)}) %copy-start.3) | copy-done | bytes 2097176
  13.2 9.6 %local.3 = (f32[256,4096]{1,0:T(8,128)S(1)}, f32[256,4096]{1,0:T(8,128)S(1)}, f32[1,4096]{1,0:T(1,128)S(1)}, f32[16,4096]{1,0:T(8,128)S(1)}, f32[1,4096]{1,0:T(1,128)S(1)}) custom-call(bf16[256,4096]{1,0:T(8,128)(2,1)S(1)} %bitcast.7, bf16[256,4096]{1,0:T(8,128)(2,1)S(1)} %bitcast.11, f32[1,4096]{1,0:T(1,128)S(1)} %reshape.71.rate_ref.refs_2_, ...), custom_call_target="tpu_custom_call" | custom-call | tf_op jit(solution)/shard_map/local/pallas_call | solution.py:326
  22.8 0.0 collective-permute-done.refs_0_.refs_5_
  22.8 0.1 multiply_add_fusion.refs_7_
  22.8 0.7 %collective-permute-start.1 = (f32[16,4096]{1,0:T(8,128)S(1)}, f32[16,4096]{1,0:T(8,128)S(1)}, u32[]{:S(2)}, u32[]{:S(2)}) collective-permute-start(f32[16,4096]{1,0:T(8,128)S(1)} %multiply_add_fusion.refs_7_), channel_id=1, source_target_pairs={{2,4},{4,2},{3,5},{5,3},{10,12},{12,10},{11,13},{13,11},{18,20},{2... | collective-permute-start | bytes 786440 | tf_op jit(solution)/shard_map/ppermute | solution.py:340
  23.5 8.0 %local.4 = (f32[256,4096]{1,0:T(8,128)S(1)}, f32[256,4096]{1,0:T(8,128)S(1)}, f32[1,4096]{1,0:T(1,128)S(1)}, f32[16,4096]{1,0:T(8,128)S(1)}, f32[1,4096]{1,0:T(1,128)S(1)}) custom-call(bf16[256,4096]{1,0:T(8,128)(2,1)S(1)} %bitcast.8, bf16[256,4096]{1,0:T(8,128)(2,1)S(1)} %bitcast.12, ...), custom_call_target="tpu_custom_call", output_to_operand_aliasing={{0}: (6, {}), {1}: (7, {}), {2}: (8, {}), {3}: (9, {}), {4}... | custom-call | tf_op jit(solution)/shard_map/local/pallas_call | solution.py:326
  31.5 0.0 collective-permute-done.1.refs_1_.refs_8_
  31.6 1.3 %collective-permute-start.2 = (f32[16,4096]{1,0:T(8,128)S(1)}, f32[16,4096]{1,0:T(8,128)S(1)}, u32[]{:S(2)}, u32[]{:S(2)}) collective-permute-start(f32[16,4096]{1,0:T(8,128)S(1)} %collective-permute-done.1.refs_1_.refs_8_), channel_id=1, source_target_pairs={{2,0},{4,6},{3,1},{5,7},{10,8},{12,14},{11,9},{13,15},{18,16},{20,... | collective-permute-start | bytes 786440 | tf_op jit(solution)/shard_map/ppermute | solution.py:340
  32.9 8.0 %local.5 = (f32[256,4096]{1,0:T(8,128)S(1)}, f32[256,4096]{1,0:T(8,128)S(1)}, f32[1,4096]{1,0:T(1,128)S(1)}, f32[16,4096]{1,0:T(8,128)S(1)}, f32[1,4096]{1,0:T(1,128)S(1)}) custom-call(bf16[256,4096]{1,0:T(8,128)(2,1)S(1)} %bitcast.9, bf16[256,4096]{1,0:T(8,128)(2,1)S(1)} %bitcast.13, ...), custom_call_target="tpu_custom_call", output_to_operand_aliasing={{0}: (6, {}), {1}: (7, {}), {2}: (8, {}), {3}: (9, {}), {4}... | custom-call | tf_op jit(solution)/shard_map/local/pallas_call | solution.py:326
  40.9 0.4 carry_grad.1
  41.3 1.6 %collective-permute-start.3 = (f32[2,4096]{1,0:T(2,128)S(1)}, f32[2,4096]{1,0:T(2,128)S(1)}, u32[]{:S(2)}, u32[]{:S(2)}) collective-permute-start(f32[2,4096]{1,0:T(2,128)S(1)} %carry_grad.1), channel_id=1, source_target_pairs={{0,8},{8,0},{16,24},{24,16},{1,9},{9,1},{17,25},{25,17},{2,10},{10... | collective-permute-start | bytes 98312 | tf_op jit(solution)/shard_map/ppermute | solution.py:394
  42.8 0.1 collective-permute-done.2.refs_2_
  43.0 1.9 %finish.4.refs_3_ = bf16[256,4096]{1,0:T(8,128)(2,1)} custom-call(f32[256,4096]{1,0:T(8,128)S(1)} %get-tuple-element.66.y_ref, f32[1,4096]{1,0:T(1,128)S(1)} %reshape.71.rate_ref.refs_2_, f32[16,4096]{1,0:T(8,128)S(1)} %get-tuple-element.42.refs_3_.wide_ref, f32[1,4096]{1,0:T(1,128)S(1)} %get-tuple-element.88.refs_4_.coef_ref, ...), custom_call_target="tpu_custom_call" | custom-call | tf_op jit(solution)/shard_map/finish/pallas_call | solution.py:377
  44.9 0.4 collective-permute-done.3
  45.3 1.6 %collective-permute-start.4 = (f32[2,4096]{1,0:T(2,128)S(1)}, f32[2,4096]{1,0:T(2,128)S(1)}, u32[]{:S(2)}, u32[]{:S(2)}) collective-permute-start(f32[2,4096]{1,0:T(2,128)S(1)} %add.16), channel_id=1, source_target_pairs={{0,16},{8,24},{16,0},{24,8},{1,17},{9,25},{17,1},{25,9},{2,18},{10... | collective-permute-start | bytes 98312 | tf_op jit(solution)/shard_map/ppermute | solution.py:394
  46.9 1.9 %finish.5 = bf16[256,4096]{1,0:T(8,128)(2,1)} custom-call(f32[256,4096]{1,0:T(8,128)S(1)} %get-tuple-element.66.y_ref, f32[1,4096]{1,0:T(1,128)S(1)} %reshape.71.rate_ref.refs_2_, f32[16,4096]{1,0:T(8,128)S(1)} %get-tuple-element.42.refs_3_.wide_ref, f32[1,4096]{1,0:T(1,128)S(1)} %get-tuple-element.88.refs_4_.coef_ref, ...), custom_call_target="tpu_custom_call", output_to_operand_aliasing={{}: (7, {})} | custom-call | tf_op jit(solution)/shard_map/finish/pallas_call | solution.py:377
  48.8 0.5 collective-permute-done.4
  49.3 4.5 %collective-permute-start.5 = (f32[2,4096]{1,0:T(2,128)S(1)}, f32[2,4096]{1,0:T(2,128)S(1)}, u32[]{:S(2)}, u32[]{:S(2)}) collective-permute-start(f32[2,4096]{1,0:T(2,128)S(1)} %add.17), channel_id=1, source_target_pairs={{0,2},{2,0},{4,6},{6,4},{1,3},{3,1},{5,7},{7,5},{8,10},{10,8},{12,... | collective-permute-start | bytes 98312 | tf_op jit(solution)/shard_map/ppermute | solution.py:394
  53.8 1.9 %finish.6.refs_3_ = bf16[256,4096]{1,0:T(8,128)(2,1)} custom-call(f32[256,4096]{1,0:T(8,128)S(1)} %get-tuple-element.74.y_ref, f32[1,4096]{1,0:T(1,128)S(1)} %reshape.71.rate_ref.refs_2_, f32[16,4096]{1,0:T(8,128)S(1)} %get-tuple-element.42.refs_3_.wide_ref, f32[1,4096]{1,0:T(1,128)S(1)} %get-tuple-element.88.refs_4_.coef_ref, ...), custom_call_target="tpu_custom_call" | custom-call | tf_op jit(solution)/shard_map/finish/pallas_call | solution.py:377
  55.7 0.0 collective-permute-done.5
  55.7 1.5 %collective-permute-start.6 = (f32[2,4096]{1,0:T(2,128)S(1)}, f32[2,4096]{1,0:T(2,128)S(1)}, u32[]{:S(2)}, u32[]{:S(2)}) collective-permute-start(f32[2,4096]{1,0:T(2,128)S(1)} %add.18), channel_id=1, source_target_pairs={{0,4},{2,6},{4,0},{6,2},{1,5},{3,7},{5,1},{7,3},{8,12},{10,14},{12... | collective-permute-start | bytes 98312 | tf_op jit(solution)/shard_map/ppermute | solution.py:394
  57.2 1.9 %finish.7 = bf16[256,4096]{1,0:T(8,128)(2,1)} custom-call(f32[256,4096]{1,0:T(8,128)S(1)} %get-tuple-element.74.y_ref, f32[1,4096]{1,0:T(1,128)S(1)} %reshape.71.rate_ref.refs_2_, f32[16,4096]{1,0:T(8,128)S(1)} %get-tuple-element.42.refs_3_.wide_ref, f32[1,4096]{1,0:T(1,128)S(1)} %get-tuple-element.88.refs_4_.coef_ref, ...), custom_call_target="tpu_custom_call", output_to_operand_aliasing={{}: (7, {})} | custom-call | tf_op jit(solution)/shard_map/finish/pallas_call | solution.py:377
  59.1 1.5 %collective-permute-done.6 = f32[2,4096]{1,0:T(2,128)S(1)} collective-permute-done((f32[2,4096]{1,0:T(2,128)S(1)}, f32[2,4096]{1,0:T(2,128)S(1)}, u32[]{:S(2)}, u32[]{:S(2)}) %collective-permute-start.6) | collective-permute-done | bytes 32800 | tf_op jit(solution)/shard_map/ppermute | solution.py:394
  60.6 0.6 %fusion.1 = (f32[1,4096]{1,0:T(1,128)}, f32[4096]{0:T(1024)S(1)}) fusion(f32[2,4096]{1,0:T(2,128)S(1)} %add.19), kind=kLoop, calls=%fused_computation.4 | loop fusion | bytes 65536 | tf_op jit(solution)/shard_map/slice | solution.py:406
  61.3 0.1 reshape_squeeze.3
  61.4 0.7 %copy.26 = f32[256,16]{0,1:T(8,128)} copy(f32[256,16]{1,0:T(8,128)S(1)} %reshape_squeeze.3) | data formatting | bytes 32768
  (4 shorter events, 0.1 us)
Async XLA Ops:
  0.6 10.7 %copy-start.5 = (f32[256,16]{0,1:T(8,128)S(1)}, f32[256,16]{0,1:T(8,128)}, u32[]{:S(2)}) copy-start(f32[256,16]{0,1:T(8,128)} %param.7) | copy-start | bytes 49156
  0.6 10.9 %copy-start.4 = (f32[4096]{0:T(1024)S(1)}, f32[4096]{0:T(1024)}, u32[]{:S(2)}) copy-start(f32[4096]{0:T(1024)} %param.9) | copy-start | bytes 49156
  1.6 1.6 %copy-start = (bf16[1,256,4096]{2,1,0:T(8,128)(2,1)S(1)}, bf16[1,256,4096]{2,1,0:T(8,128)(2,1)}, u32[]{:S(2)}) copy-start(bf16[1,256,4096]{2,1,0:T(8,128)(2,1)} %param.5) | copy-start | bytes 6291460
  3.2 1.6 %copy-start.2 = (bf16[1,256,4096]{2,1,0:T(8,128)(2,1)S(1)}, bf16[1,256,4096]{2,1,0:T(8,128)(2,1)}, u32[]{:S(2)}) copy-start(bf16[1,256,4096]{2,1,0:T(8,128)(2,1)} %param.6) | copy-start | bytes 6291460
  4.8 6.8 %copy-start.1 = (bf16[1,256,4096]{2,1,0:T(8,128)(2,1)S(1)}, bf16[1,256,4096]{2,1,0:T(8,128)(2,1)}, u32[]{:S(2)}) copy-start(bf16[1,256,4096]{2,1,0:T(8,128)(2,1)} %param.5) | copy-start | bytes 6291460
  8.2 14.6 %collective-permute-start = (f32[16,4096]{1,0:T(8,128)S(1)}, f32[16,4096]{1,0:T(8,128)S(1)}, u32[]{:S(2)}, u32[]{:S(2)}) collective-permute-start(f32[16,4096]{1,0:T(8,128)S(1)} %get-tuple-element.49.refs_6_), channel_id=1, source_target_pairs={{0,2},{2,0},{4,6},{6,4},{1,3},{3,1},{5,7},{7,5},{8,10},{10,8},{12,... | collective-permute-start | bytes 786440 | tf_op jit(solution)/shard_map/ppermute | solution.py:340
  11.6 1.6 %copy-start.3 = (bf16[1,256,4096]{2,1,0:T(8,128)(2,1)S(1)}, bf16[1,256,4096]{2,1,0:T(8,128)(2,1)}, u32[]{:S(2)}) copy-start(bf16[1,256,4096]{2,1,0:T(8,128)(2,1)} %param.6) | copy-start | bytes 6291460
  22.8 8.7 %collective-permute-start.1 = (f32[16,4096]{1,0:T(8,128)S(1)}, f32[16,4096]{1,0:T(8,128)S(1)}, u32[]{:S(2)}, u32[]{:S(2)}) collective-permute-start(f32[16,4096]{1,0:T(8,128)S(1)} %multiply_add_fusion.refs_7_), channel_id=1, source_target_pairs={{2,4},{4,2},{3,5},{5,3},{10,12},{12,10},{11,13},{13,11},{18,20},{2... | collective-permute-start | bytes 786440 | tf_op jit(solution)/shard_map/ppermute | solution.py:340
  31.6 11.4 %collective-permute-start.2 = (f32[16,4096]{1,0:T(8,128)S(1)}, f32[16,4096]{1,0:T(8,128)S(1)}, u32[]{:S(2)}, u32[]{:S(2)}) collective-permute-start(f32[16,4096]{1,0:T(8,128)S(1)} %collective-permute-done.1.refs_1_.refs_8_), channel_id=1, source_target_pairs={{2,0},{4,6},{3,1},{5,7},{10,8},{12,14},{11,9},{13,15},{18,16},{20,... | collective-permute-start | bytes 786440 | tf_op jit(solution)/shard_map/ppermute | solution.py:340
  41.3 4.0 %collective-permute-start.3 = (f32[2,4096]{1,0:T(2,128)S(1)}, f32[2,4096]{1,0:T(2,128)S(1)}, u32[]{:S(2)}, u32[]{:S(2)}) collective-permute-start(f32[2,4096]{1,0:T(2,128)S(1)} %carry_grad.1), channel_id=1, source_target_pairs={{0,8},{8,0},{16,24},{24,16},{1,9},{9,1},{17,25},{25,17},{2,10},{10... | collective-permute-start | bytes 98312 | tf_op jit(solution)/shard_map/ppermute | solution.py:394
  45.3 4.0 %collective-permute-start.4 = (f32[2,4096]{1,0:T(2,128)S(1)}, f32[2,4096]{1,0:T(2,128)S(1)}, u32[]{:S(2)}, u32[]{:S(2)}) collective-permute-start(f32[2,4096]{1,0:T(2,128)S(1)} %add.16), channel_id=1, source_target_pairs={{0,16},{8,24},{16,0},{24,8},{1,17},{9,25},{17,1},{25,9},{2,18},{10... | collective-permute-start | bytes 98312 | tf_op jit(solution)/shard_map/ppermute | solution.py:394
  49.3 6.4 %collective-permute-start.5 = (f32[2,4096]{1,0:T(2,128)S(1)}, f32[2,4096]{1,0:T(2,128)S(1)}, u32[]{:S(2)}, u32[]{:S(2)}) collective-permute-start(f32[2,4096]{1,0:T(2,128)S(1)} %add.17), channel_id=1, source_target_pairs={{0,2},{2,0},{4,6},{6,4},{1,3},{3,1},{5,7},{7,5},{8,10},{10,8},{12,... | collective-permute-start | bytes 98312 | tf_op jit(solution)/shard_map/ppermute | solution.py:394
  55.7 4.9 %collective-permute-start.6 = (f32[2,4096]{1,0:T(2,128)S(1)}, f32[2,4096]{1,0:T(2,128)S(1)}, u32[]{:S(2)}, u32[]{:S(2)}) collective-permute-start(f32[2,4096]{1,0:T(2,128)S(1)} %add.18), channel_id=1, source_target_pairs={{0,4},{2,6},{4,0},{6,2},{1,5},{3,7},{5,1},{7,3},{8,12},{10,14},{12... | collective-permute-start | bytes 98312 | tf_op jit(solution)/shard_map/ppermute | solution.py:394

commit v2 on v1

v2 whole, which is shorter than its diff:
```python
import functools
import math

import jax
import jax.numpy as jnp
from jax import lax
from jax.experimental import pallas as pl
from jax.experimental.pallas import tpu as pltpu
from jax.sharding import PartitionSpec as P


f32 = jnp.float32
bf16 = jnp.bfloat16
LANES = 128
TILES_A, TILES_B, TILES_C = 8, 4, 8
VMEM_LIMIT = 16 * 2**20
CUTS = (6, 12)


def split(value):
    high = value.astype(bf16)
    low = (value - high.astype(f32)).astype(bf16)
    return high, low


def mm(left, right):
    return lax.dot_general(left, right, (((1,), (0,)), ((), ())), preferred_element_type=f32)


def iota(shape, axis):
    return lax.broadcasted_iota(jnp.int32, shape, axis)


def lanes_of(k, tiles, first=0):
    return pl.ds(pl.multiple_of((pl.program_id(0) + first) * (tiles * LANES) + k * LANES, LANES), LANES)


def sel_rows(full, block, owner):
    total = full[0:block]
    for g in range(1, full.shape[0] // block):
        total = jnp.where(owner == g, full[g * block : (g + 1) * block], total)
    return total


def stack(parts, axis):
    return jnp.concatenate(parts, axis=axis)


def column(row, eye):
    return jnp.sum(jnp.where(eye, row, 0.0), axis=1, keepdims=True)


def halves(value, size):
    return value[:size] + value[size:]


def three(table_h, table_l, right_h, right_l):
    left = stack([stack([table_h, table_h], 1), stack([table_l, jnp.zeros_like(table_l)], 1)], 0)
    return halves(mm(left, stack([right_h, right_l], 0)), table_h.shape[0])


def chunk_of(width, modes):
    return max(1, 2 * width // modes) * modes


def block_mask(width, modes):
    sq = (LANES, LANES)
    return ((iota(sq, 0) // modes) == (iota(sq, 1) // width)).astype(bf16)


def ends_kernel(width, modes, tiles, x_ref, d_ref, rates_ref, residues_ref, near_ref, far_ref, wide_ref, x_out, d_out, rate_out, coef_out, weight_out):
    rows = x_ref.shape[0]
    groups = LANES // width
    sq = (LANES, LANES)
    eye = iota(sq, 0) == iota(sq, 1)
    member = (iota(sq, 0) == iota(sq, 1) // width).astype(bf16)
    owner = iota((modes, LANES), 1) // width
    pick = iota((modes, LANES), 0) == iota((modes, LANES), 1) % width
    spot = iota(sq, 1).astype(f32)
    even = lax.axis_index("ctx") % 2 == 0
    pieces = rows // LANES
    gathered = []
    for k in range(tiles):
        group = (pl.program_id(0) * tiles + k) * groups
        home = pl.ds(pl.multiple_of(group // LANES * LANES, LANES), LANES)
        turn = (LANES - group % LANES) % LANES
        for ref in (rates_ref, residues_ref):
            value = pltpu.roll(ref[:, home], turn, 1)
            a = value.astype(bf16)
            rest = value - a.astype(f32)
            b = rest.astype(bf16)
            gathered += [a, b, (rest - b.astype(f32)).astype(bf16)]
    spread = mm(stack(gathered, 0), member)
    for k in range(tiles):
        here, lanes = slice(k * LANES, (k + 1) * LANES), lanes_of(k, tiles)
        parts = [spread[(6 * k + n) * modes : (6 * k + n + 1) * modes] for n in range(6)]
        wide, mixed = parts[0] + parts[1] + parts[2], parts[3] + parts[4] + parts[5]
        row = jnp.sum(jnp.where(pick, wide, 0.0), axis=0, keepdims=True)
        weight = jnp.sqrt(1.0 - jnp.exp(-2.0 * row))
        rate_out[:, lanes] = row
        weight_out[:, lanes] = weight
        coef_out[:, lanes] = jnp.sum(jnp.where(pick, mixed, 0.0), axis=0, keepdims=True) * weight
        wide_ref[:, lanes] = wide
        rate = column(row, eye)
        step = jnp.exp(-wide * float(LANES))
        got = []
        for power, src, out in ((LANES - 1.0 - spot, x_ref, x_out), (spot, d_ref, d_out)):
            high, low = split(jnp.exp(-rate * power))
            out[:, lanes] = src[:, here]
            flat = stack([src[h * LANES : (h + 1) * LANES, here] for h in range(pieces)], 1)
            full = mm(stack([high, low], 1), stack([flat, flat], 0))
            got.append([sel_rows(full[:, h * LANES : (h + 1) * LANES], modes, owner) for h in range(pieces)])
        end = got[0][0]
        for h in range(1, pieces):
            end = end * step + got[0][h]
        start = got[1][pieces - 1]
        for h in range(pieces - 2, -1, -1):
            start = start * step + got[1][h]
        near_ref[:, lanes] = jnp.where(even, end, start)
        far_ref[:, lanes] = jnp.where(even, start, end)


def local_kernel(width, modes, tiles, begin, *refs):
    x_ref, d_ref, rate_ref, wide_ref, coef_ref, skip_ref = refs[:6]
    yx_ref, yd_ref, sx_ref, sd_ref, grad_ref, far_ref, gskip_ref, own_ref = refs[-8:]
    rows = x_ref.shape[0]
    groups = LANES // width
    chunk = chunk_of(width, modes)
    fold = chunk // modes
    count = rows // chunk

    @pl.when(pl.program_id(0) == 0)
    def _():
        own_ref[...] = block_mask(width, modes)

    own = own_ref[...]
    owner = iota((chunk, LANES), 1) // width
    flat = (chunk, fold * LANES)
    t_int = iota(flat, 0)
    s_int = iota(flat, 1) // LANES * modes + iota(flat, 1) % modes
    spot = iota((chunk, LANES), 0).astype(f32)
    place = iota((modes, LANES), 1) % modes

    def spread(compact):
        return stack([compact] * groups, 0) * own

    def tall(compact):
        return stack([spread(compact[f * modes : (f + 1) * modes]) for f in range(fold)], 0)

    def broad(compact):
        return stack([spread(compact[:, f * LANES : (f + 1) * LANES]) for f in range(fold)], 1)

    def tables(lanes):
        row, coef, wide = rate_ref[:, lanes], coef_ref[:, lanes], wide_ref[:, lanes]
        down = jnp.exp(-row * spot)
        up = jnp.exp(row * spot)
        first = split(down * (coef * jnp.exp(row * (chunk - 1.0))))
        last = split(up * coef)
        start = split(stack([jnp.exp(-wide * (place + f * modes).astype(f32)) for f in range(fold)], 1))
        end = split(stack([jnp.exp(-wide * (chunk - 1 - f * modes - place).astype(f32)) for f in range(fold)], 1))
        forth = jnp.where(t_int >= s_int, three(*first, broad(end[0]), broad(end[1])), 0.0)
        back = jnp.where(t_int <= s_int, three(*last, broad(start[0]), broad(start[1])), 0.0)
        x_left = stack([*split(forth), *end], 0)
        d_left = stack([*split(back), *start], 0)
        return down, split(up), x_left, d_left

    def tiles_of(src, lanes):
        expanded = [tall(src[j * chunk : (j + 1) * chunk, lanes]) for j in range(count)]
        return [stack(expanded[j : j + 2], 1) for j in range(0, count, 2)]

    def near_part(left, right, src, dst, lanes):
        skip = skip_ref[:, lanes]
        found = []
        for p, block in enumerate(right):
            res = mm(left, block)
            own_part = halves(res[: 2 * chunk], chunk)
            ends = halves(res[2 * chunk :], modes)
            for q in range(2):
                half = slice(q * LANES, (q + 1) * LANES)
                spots = slice((2 * p + q) * chunk, (2 * p + q + 1) * chunk)
                dst[spots, lanes] = own_part[:, half] + skip * src[spots, lanes].astype(f32)
                found.append(ends[:, half])
        return found

    def near_grad(right, lanes):
        return lax.dot_general(
            stack([d_ref[j * chunk : (j + 1) * chunk, lanes] for j in range(count)], 1),
            stack(right, 1),
            (((1,), (1,)), ((), ())),
            preferred_element_type=f32,
        )

    def scans(ends_x, starts_d, lanes):
        wide = wide_ref[:, lanes]
        leap = jnp.exp(-wide * float(chunk))
        state = far = jnp.zeros((modes, LANES), f32)
        for j in range(count):
            sx_ref[j * modes : (j + 1) * modes, lanes] = state
            far = far + starts_d[j] * state
            state = (state + ends_x[j]) * leap
        far_ref[:, lanes] = far * jnp.exp(wide * float(chunk))
        state = jnp.zeros((modes, LANES), f32)
        for j in range(count - 1, -1, -1):
            sd_ref[j * modes : (j + 1) * modes, lanes] = state
            state = (state + starts_d[j]) * leap

    def skip_grad(lanes):
        total = jnp.zeros((chunk, LANES), f32)
        for j in range(count):
            spots = slice(j * chunk, (j + 1) * chunk)
            total = total + x_ref[spots, lanes].astype(f32) * d_ref[spots, lanes].astype(f32)
        gskip_ref[:, lanes] = jnp.sum(total, axis=0, keepdims=True)

    def finish_grad(pairs, down, up, lanes):
        parts = split(jnp.where(t_int >= s_int, pairs, 0.0))
        res = mm(stack(parts, 0), stack([tall(up[0]), tall(up[1])], 1))
        near = res[:chunk, :LANES] + res[:chunk, LANES:] + res[chunk:, :LANES]
        grad_ref[:, lanes] = jnp.sum(near * down, axis=0, keepdims=True)

    spans = [lanes_of(k, tiles, begin) for k in range(tiles)]
    ready = tables(spans[0])
    held = None
    for k, lanes in enumerate(spans):
        down, up, x_left, d_left = ready
        x_right = tiles_of(x_ref, lanes)
        ends_x = near_part(x_left, x_right, x_ref, yx_ref, lanes)
        pairs = near_grad(x_right, lanes)
        if k + 1 < tiles:
            ready = tables(spans[k + 1])
        starts_d = near_part(d_left, tiles_of(d_ref, lanes), d_ref, yd_ref, lanes)
        scans(ends_x, starts_d, lanes)
        skip_grad(lanes)
        if held is not None:
            finish_grad(*held)
        held = (pairs, down, up, lanes)
    finish_grad(*held)


def carry_grad_kernel(width, modes, scale, four, *refs):
    out_ref = refs[-1]
    near_ref, far_ref, rate_ref, weight_ref, skip_ref = refs[:5]
    p_ref, q_ref = refs[5:7]
    sq = (LANES, LANES)
    same = ((iota(sq, 0) // width) == (iota(sq, 1) // width)).astype(bf16)
    pick = iota((modes, LANES), 0) == iota((modes, LANES), 1) % modes
    place = lax.axis_index("ctx")
    inner = ((place == 1) | (place == 2)).astype(f32)
    middle = (place == 1).astype(f32)
    for k in range(p_ref.shape[1] // LANES):
        lanes = slice(k * LANES, (k + 1) * LANES)
        value = p_ref[:, lanes] * q_ref[:, lanes]
        if four:
            r_ref, s_ref = refs[7:9]
            value = value * inner + r_ref[:, lanes] * s_ref[:, lanes] * middle
        high, low = split(value + far_ref[:, lanes])
        sums = mm(stack([high, low], 1), stack([same, same], 0))
        far = jnp.sum(jnp.where(pick, sums, 0.0), axis=0, keepdims=True)
        out_ref[0:1, lanes] = (near_ref[:, lanes] + far * jnp.exp(-rate_ref[:, lanes])) * (weight_ref[:, lanes] * scale)
        out_ref[1:2, lanes] = skip_ref[:, lanes] * scale


def finish_kernel(width, modes, tiles, begin, forward, four, y_ref, held_ref, rate_ref, wide_ref, coef_ref, *refs):
    o_ref = refs[-1]
    rows = y_ref.shape[0]
    groups = LANES // width
    chunk = chunk_of(width, modes)
    count = rows // chunk
    own = block_mask(width, modes)
    spot = iota((chunk, LANES), 0).astype(f32)
    place = lax.axis_index("ctx")
    if not forward:
        place = 3 - place

    def spread(compact):
        return stack([compact] * groups, 0) * own

    for k in range(tiles):
        here, lanes = slice(k * LANES, (k + 1) * LANES), lanes_of(k, tiles, begin)
        row, coef, wide = rate_ref[:, lanes], coef_ref[:, lanes], wide_ref[:, lanes]
        leap = jnp.exp(-wide * float(chunk))
        state = refs[0][:, lanes]
        if four:
            both = state + refs[2][:, lanes] * jnp.exp(-wide * float(rows))
            state = jnp.where(place == 0, 0.0, jnp.where(place == 2, refs[1][:, lanes], both))
        table = coef * jnp.exp(row * ((chunk - 1.0) - spot if forward else spot))
        table = split(table)
        parts = [None] * count
        for j in range(count) if forward else range(count - 1, -1, -1):
            state = state * leap
            parts[j] = split(state + held_ref[j * modes : (j + 1) * modes, lanes])
        for p in range(0, count, 2):
            pair = parts[p : p + 2]
            res = three(*table, stack([spread(h) for h, _ in pair], 1), stack([spread(l) for _, l in pair], 1))
            for q in range(2):
                spots = slice((p + q) * chunk, (p + q + 1) * chunk)
                o_ref[spots, here] = (y_ref[spots, lanes] + res[:, q * LANES : (q + 1) * LANES]).astype(bf16)


def swap_states(near, far, power, even, count):
    end, start = jnp.where(even, near, far), jnp.where(even, far, near)
    before, after, prior, distance = end, start, None, 1
    have_x, have_d = None, None
    while distance < count:
        got_x = lax.ppermute(before, "ctx", [(i, i + distance) for i in range(count - distance)])
        got_d = lax.ppermute(after, "ctx", [(i + distance, i) for i in range(count - distance)])
        have_x = got_x if prior is None else have_x + prior * got_x
        have_d = got_d if prior is None else have_d + prior * got_d
        prior = power if prior is None else prior * power
        before, after = before + power * got_x, after + power * got_d
        power = power * power
        distance *= 2
    return have_x, have_d, start


def layer(inputs, cotangent, residues, decay_rates, skip_gain):
    local_batch, rows, channels = inputs.shape
    group_count, modes = residues.shape
    width = channels // group_count
    x, d = inputs.reshape(local_batch * rows, channels), cotangent.reshape(local_batch * rows, channels)
    rates, mixing = decay_rates.T, residues.T
    if group_count % LANES:
        rates, mixing = (jnp.pad(v, ((0, 0), (0, -group_count % LANES))) for v in (rates, mixing))
    skip = skip_gain.reshape(1, channels)
    count = lax.axis_size("ctx")
    four = count == 4
    blocks = channels // LANES
    every = pl.BlockSpec(memory_space=pl.ANY)
    params = pltpu.CompilerParams(vmem_limit_bytes=VMEM_LIMIT)

    whole = pl.BlockSpec(memory_space=pltpu.VMEM)

    def block(tiles, offset=0):
        return pl.BlockSpec((rows, tiles * LANES), lambda i: (0, i + offset))

    tiles = math.gcd(TILES_A, blocks)
    x, d = (pltpu.with_memory_space_constraint(value, pltpu.HBM) for value in (x, d))
    near, far, wide, x, d, rate, coef, weight = pl.pallas_call(
        functools.partial(ends_kernel, width, modes, tiles),
        grid=(blocks // tiles,),
        in_specs=[block(tiles), block(tiles), whole, whole],
        out_specs=[whole] * 8,
        out_shape=[jax.ShapeDtypeStruct((modes, channels), f32)] * 3
        + [jax.ShapeDtypeStruct((rows, channels), bf16)] * 2
        + [jax.ShapeDtypeStruct((1, channels), f32)] * 3,
        compiler_params=params,
        name="ends",
    )(x, d, rates, mixing)
    power = jnp.exp(-wide * float(rows))

    tiles_b = math.gcd(TILES_B, blocks)
    steps = blocks // tiles_b
    held = rows // chunk_of(width, modes) * modes

    def local(first, size, past):
        return pl.pallas_call(
            functools.partial(local_kernel, width, modes, tiles_b, first),
            grid=(size,),
            in_specs=[whole] * (6 if past is None else 13),
            out_specs=[whole] * 7,
            out_shape=[jax.ShapeDtypeStruct((rows, channels), f32)] * 2
            + [jax.ShapeDtypeStruct((size_of, channels), f32) for size_of in (held, held, 1, modes, 1)],
            scratch_shapes=[pltpu.VMEM((LANES, LANES), bf16)],
            input_output_aliases={} if past is None else {6 + n: n for n in range(7)},
            compiler_params=params,
            name="local",
        )(x, d, rate, wide, coef, skip, *(past or ()))

    def swap(value, pairs):
        return lax.ppermute(value, "ctx", pairs)

    if four:
        one = swap(near, [(0, 1), (1, 0), (2, 3), (3, 2)])
        cut_a, cut_b = max(1, steps * CUTS[0] // 16), max(2, steps * CUTS[1] // 16)
        past = local(0, cut_a, None)
        meet = far + power * one
        past, meet = lax.optimization_barrier((past, meet))
        two = swap(meet, [(1, 2), (2, 1)])
        past = local(cut_a, cut_b - cut_a, past)
        past, two = lax.optimization_barrier((past, two))
        three = swap(two, [(1, 0), (2, 3)])
        y_x, y_d, s_x, s_d, grad, far_grad, gskip = local(cut_b, steps - cut_b, past)
        states_x = states_d = (one, two, three)
        factors = (one, near, meet, two)
    else:
        even = lax.axis_index("ctx") % 2 == 0
        have_x, have_d, start = swap_states(near, far, power, even, count)
        y_x, y_d, s_x, s_d, grad, far_grad, gskip = local(0, steps, None)
        states_x, states_d = (have_x,), (have_d,)
        factors = (have_x, start)

    token_total = local_batch * rows * lax.axis_size("dp") * count
    grads = pl.pallas_call(
        functools.partial(carry_grad_kernel, width, modes, 1.0 / math.sqrt(token_total), four),
        in_specs=[pl.BlockSpec(memory_space=pltpu.VMEM)] * (5 + len(factors)),
        out_shape=jax.ShapeDtypeStruct((2, channels), f32),
        compiler_params=params,
        name="carry_grad",
    )(grad, far_grad, rate, weight, gskip, *factors)

    tiles_c = math.gcd(TILES_C, blocks)
    steps = blocks // tiles_c

    def finish(forward, first, size, past):
        y, inner, states = (y_x, s_x, states_x) if forward else (y_d, s_d, states_d)
        return pl.pallas_call(
            functools.partial(finish_kernel, width, modes, tiles_c, first, forward, four),
            grid=(size,),
            in_specs=[whole] * (5 + len(states)) + ([] if past is None else [every]),
            out_specs=block(tiles_c, first),
            out_shape=jax.ShapeDtypeStruct((rows, channels), bf16),
            input_output_aliases={} if past is None else {5 + len(states): 0},
            compiler_params=params,
            name="finish",
        )(y, inner, rate, wide, coef, *states, *(() if past is None else (past,)))

    results = {True: None, False: None}
    queue = [(True, 0, steps // 2), (True, steps // 2, steps - steps // 2)]
    queue += [(False, 0, steps // 2), (False, steps // 2, steps - steps // 2)]
    queue = [piece for piece in queue if piece[2] > 0]
    rounds = [("dp", k) for k in doubling(lax.axis_size("dp"))] + [("ctx", k) for k in doubling(count)]
    for axis, k in rounds:
        other = lax.ppermute(grads, axis, [(i, i ^ k) for i in range(lax.axis_size(axis))])
        if queue:
            forward, first, size = queue.pop(0)
            results[forward] = finish(forward, first, size, results[forward])
            results[forward], other = lax.optimization_barrier((results[forward], other))
        grads = grads + other
    for forward, first, size in queue:
        results[forward] = finish(forward, first, size, results[forward])
    return (
        results[True].reshape(inputs.shape),
        results[False].reshape(inputs.shape),
        grads[0].reshape(group_count, modes),
        grads[1],
    )


def doubling(size):
    return [1 << n for n in range(size.bit_length() - 1)]


def solution(mesh):
    placed = (P("dp", "ctx", "tp"), P("dp", "ctx", "tp"), P("tp", None), P("tp", None), P("tp"))
    return jax.shard_map(
        layer,
        mesh=mesh,
        in_specs=placed,
        out_specs=(P("dp", "ctx", "tp"), P("dp", "ctx", "tp"), P("tp", None), P("tp")),
        check_vma=False,
    )
```

time: 62.3 us -> 52.7 us (0.85)
  Pallas kernels: 37.1 us -> 32 us
  local copies, waits for them, and re-layouts: 7.33 us -> 2.84 us
  starting transfers between devices: 14.2 us -> 10.8 us
  waiting for transfers between devices: 2.46 us -> 5.85 us
    pallas_call x7, Pallas kernels: 33.3 us -> 25.8 us  [the longest x3 15.6 us: local(): pl.pallas_call(functools.partial(local_kernel, width, modes, tiles_b, fir...]
    unnamed x15 -> x7, local copies, waits for them, and re-layouts: 6.38 us -> 2.11 us
    ppermute x3, waiting for transfers between devices: 0.12 us -> 4.1 us  [swap(): return lax.ppermute(value, 'ctx', pairs)]
    ppermute x4, starting transfers between devices: 9.1 us -> 5.68 us  [layer(): lax.ppermute(grads, axis, [(i, i ^ k) for i in range(lax.axis_size(axis))])]
    pallas_call x1, Pallas kernels: 3.37 us -> 5.81 us  [layer(): pl.pallas_call(functools.partial(ends_kernel, width, modes, tiles), grid=...]
  transfers between devices with their start and end apart: 7 -> 7, of which waited for: 4 -> 4; matrix products, arithmetic and copies ran while one was open for 0% -> 0% of each run, Pallas kernels for 54% -> 50%
where the time goes in v2:
time: 52.7 us; the launch traced here: 52.4 us
  Pallas kernels  32 us (61%)
  starting transfers between devices  10.8 us (20%)
  waiting for transfers between devices  5.85 us (11%)
  local copies, waits for them, and re-layouts  2.84 us (5%)
  between operations  0.74 us (1%)
    pallas_call x3, Pallas kernels, local(): pl.pallas_call(functools.partial(local_kernel, width, modes, tiles_b, fir...  15.6 us
    pallas_call x4, Pallas kernels, finish(): pl.pallas_call(functools.partial(finish_kernel, width, modes, tiles_c, fi...  10.2 us
    pallas_call x1, Pallas kernels, layer(): pl.pallas_call(functools.partial(ends_kernel, width, modes, tiles), grid=...  5.81 us
    ppermute x4, starting transfers between devices, layer(): lax.ppermute(grads, axis, [(i, i ^ k) for i in range(lax.axis_size(axis))])  5.68 us
    ppermute x3, starting transfers between devices, swap(): return lax.ppermute(value, 'ctx', pairs)  5.08 us
    ppermute x3, waiting for transfers between devices, swap(): return lax.ppermute(value, 'ctx', pairs)  4.1 us
    unnamed x7, local copies, waits for them, and re-layouts  2.11 us
    ppermute x4, waiting for transfers between devices, layer(): lax.ppermute(grads, axis, [(i, i ^ k) for i in range(lax.axis_size(axis))])  1.76 us
  transfers between devices with their start and end apart: 7, of which 4 were waited for; matrix products, arithmetic and copies ran while one was open for 0% of the time, Pallas kernels for 50%

profile of v2, /device:TPU:0, one launch (start us, length us, event | category | flops | bytes accessed | tf_op | source)
XLA Modules:
  0.0 52.4 jit_solution(13617631100396004024)
XLA Ops:
  0.6 0.0 copy-start.1
  0.6 0.7 %copy-done.1 = f32[256,16]{0,1:T(8,128)S(1)} copy-done((f32[256,16]{0,1:T(8,128)S(1)}, f32[256,16]{0,1:T(8,128)}, u32[]{:S(2)}) %copy-start.1) | copy-done | bytes 16408
  1.4 0.0 copy-start.2
  1.4 0.7 %copy-done.2 = f32[256,16]{0,1:T(8,128)S(1)} copy-done((f32[256,16]{0,1:T(8,128)S(1)}, f32[256,16]{0,1:T(8,128)}, u32[]{:S(2)}) %copy-start.2) | copy-done | bytes 16408
  2.1 0.0 copy-start
  2.1 5.8 %ends.1 = (f32[16,4096]{1,0:T(8,128)S(1)}, f32[16,4096]{1,0:T(8,128)S(1)}, f32[16,4096]{1,0:T(8,128)S(1)}, bf16[256,4096]{1,0:T(8,128)(2,1)S(1)}, bf16[256,4096]...) custom-call(bf16[256,4096]{1,0:T(8,128)(2,1)} %bitcast.15, ...), custom_call_target="tpu_custom_call" | custom-call | tf_op jit(solution)/shard_map/ends/pallas_call | solution.py:337
  7.9 3.1 %collective-permute-start = (f32[16,4096]{1,0:T(8,128)S(1)}, f32[16,4096]{1,0:T(8,128)S(1)}, u32[]{:S(2)}, u32[]{:S(2)}) collective-permute-start(f32[16,4096]{1,0:T(8,128)S(1)} %get-tuple-element.70.refs_6_), channel_id=1, source_target_pairs={{0,2},{2,0},{4,6},{6,4},{1,3},{3,1},{5,7},{7,5},{8,10},{10,8},{12,... | collective-permute-start | bytes 786440 | tf_op jit(solution)/shard_map/ppermute | solution.py:369
  11.0 0.0 copy-done
  11.0 5.8 %local.3 = (f32[256,4096]{1,0:T(8,128)S(1)}, f32[256,4096]{1,0:T(8,128)S(1)}, f32[128,4096]{1,0:T(8,128)S(1)}, f32[128,4096]{1,0:T(8,128)S(1)}, f32[1,4096]{1,0:...) custom-call(bf16[256,4096]{1,0:T(8,128)(2,1)S(1)} %get-tuple-element.57.refs_0_, ...), custom_call_target="tpu_custom_call" | custom-call | tf_op jit(solution)/shard_map/local/pallas_call | solution.py:355
  16.8 0.5 collective-permute-done.refs_0_.refs_5_
  17.3 0.1 multiply_add_fusion.refs_7_
  17.4 0.7 %collective-permute-start.1 = (f32[16,4096]{1,0:T(8,128)S(1)}, f32[16,4096]{1,0:T(8,128)S(1)}, u32[]{:S(2)}, u32[]{:S(2)}) collective-permute-start(f32[16,4096]{1,0:T(8,128)S(1)} %multiply_add_fusion.refs_7_), channel_id=1, source_target_pairs={{2,4},{4,2},{3,5},{5,3},{10,12},{12,10},{11,13},{13,11},{18,20},{2... | collective-permute-start | bytes 786440 | tf_op jit(solution)/shard_map/ppermute | solution.py:369
  18.1 5.9 %local.4 = (f32[256,4096]{1,0:T(8,128)S(1)}, f32[256,4096]{1,0:T(8,128)S(1)}, f32[128,4096]{1,0:T(8,128)S(1)}, f32[128,4096]{1,0:T(8,128)S(1)}, f32[1,4096]{1,0:...) custom-call(bf16[256,4096]{1,0:T(8,128)(2,1)S(1)} %get-tuple-element, ...), custom_call_target="tpu_custom_call", output_to_operand_aliasing={{0}: (6, {}), {1}: (7, {}), {2}: (8, {}), {3}: (9, {}), {4}... | custom-call | tf_op jit(solution)/shard_map/local/pallas_call | solution.py:355
  23.9 0.0 collective-permute-done.1.refs_1_.refs_8_
  23.9 1.3 %collective-permute-start.2 = (f32[16,4096]{1,0:T(8,128)S(1)}, f32[16,4096]{1,0:T(8,128)S(1)}, u32[]{:S(2)}, u32[]{:S(2)}) collective-permute-start(f32[16,4096]{1,0:T(8,128)S(1)} %collective-permute-done.1.refs_1_.refs_8_), channel_id=1, source_target_pairs={{2,0},{4,6},{3,1},{5,7},{10,8},{12,14},{11,9},{13,15},{18,16},{20,... | collective-permute-start | bytes 786440 | tf_op jit(solution)/shard_map/ppermute | solution.py:369
  25.2 3.9 %local.5 = (f32[256,4096]{1,0:T(8,128)S(1)}, f32[256,4096]{1,0:T(8,128)S(1)}, f32[128,4096]{1,0:T(8,128)S(1)}, f32[128,4096]{1,0:T(8,128)S(1)}, f32[1,4096]{1,0:...) custom-call(bf16[256,4096]{1,0:T(8,128)(2,1)S(1)} %get-tuple-element, ...), custom_call_target="tpu_custom_call", output_to_operand_aliasing={{0}: (6, {}), {1}: (7, {}), {2}: (8, {}), {3}: (9, {}), {4}... | custom-call | tf_op jit(solution)/shard_map/local/pallas_call | solution.py:355
  29.2 0.4 carry_grad.1
  29.6 1.7 %collective-permute-start.3 = (f32[2,4096]{1,0:T(2,128)S(1)}, f32[2,4096]{1,0:T(2,128)S(1)}, u32[]{:S(2)}, u32[]{:S(2)}) collective-permute-start(f32[2,4096]{1,0:T(2,128)S(1)} %carry_grad.1), channel_id=1, source_target_pairs={{0,8},{8,0},{16,24},{24,16},{1,9},{9,1},{17,25},{25,17},{2,10},{10... | collective-permute-start | bytes 98312 | tf_op jit(solution)/shard_map/ppermute | solution.py:422
  31.3 3.6 %collective-permute-done.2.refs_2_ = f32[16,4096]{1,0:T(8,128)S(1)} collective-permute-done((f32[16,4096]{1,0:T(8,128)S(1)}, f32[16,4096]{1,0:T(8,128)S(1)}, u32[]{:S(2)}, u32[]{:S(2)}) %collective-permute-start.2) | collective-permute-done | bytes 262176 | tf_op jit(solution)/shard_map/ppermute | solution.py:369
  34.9 2.6 %finish.4.refs_3_ = bf16[256,4096]{1,0:T(8,128)(2,1)} custom-call(f32[256,4096]{1,0:T(8,128)S(1)} %get-tuple-element.93.y_ref, f32[128,4096]{1,0:T(8,128)S(1)} %get-tuple-element.94.held_ref, f32[1,4096]{1,0:T(1,128)S(1)} %get-tuple-element.59.refs_2_.rate_ref, f32[16,4096]{1,0:T(8,128)S(1)} %get-tuple-element.60.refs_3_.wide_ref, ...), custom_call_target="tpu_custom_call" | custom-call | tf_op jit(solution)/shard_map/finish/pallas_call | solution.py:405
  37.5 0.0 collective-permute-done.3
  37.5 1.6 %collective-permute-start.4 = (f32[2,4096]{1,0:T(2,128)S(1)}, f32[2,4096]{1,0:T(2,128)S(1)}, u32[]{:S(2)}, u32[]{:S(2)}) collective-permute-start(f32[2,4096]{1,0:T(2,128)S(1)} %add.16), channel_id=1, source_target_pairs={{0,16},{8,24},{16,0},{24,8},{1,17},{9,25},{17,1},{25,9},{2,18},{10... | collective-permute-start | bytes 98312 | tf_op jit(solution)/shard_map/ppermute | solution.py:422
  39.1 2.6 %finish.5 = bf16[256,4096]{1,0:T(8,128)(2,1)} custom-call(f32[256,4096]{1,0:T(8,128)S(1)} %get-tuple-element.93.y_ref, f32[128,4096]{1,0:T(8,128)S(1)} %get-tuple-element.94.held_ref, f32[1,4096]{1,0:T(1,128)S(1)} %get-tuple-element.59.refs_2_.rate_ref, f32[16,4096]{1,0:T(8,128)S(1)} %get-tuple-element.60.refs_3_.wide_ref, ...), custom_call_target="tpu_custom_call", output_to_operand_aliasing={{}: (8, {})} | custom-call | tf_op jit(solution)/shard_map/finish/pallas_call | solution.py:405
  41.7 0.0 collective-permute-done.4
  41.7 0.8 %collective-permute-start.5 = (f32[2,4096]{1,0:T(2,128)S(1)}, f32[2,4096]{1,0:T(2,128)S(1)}, u32[]{:S(2)}, u32[]{:S(2)}) collective-permute-start(f32[2,4096]{1,0:T(2,128)S(1)} %add.17), channel_id=1, source_target_pairs={{0,2},{2,0},{4,6},{6,4},{1,3},{3,1},{5,7},{7,5},{8,10},{10,8},{12,... | collective-permute-start | bytes 98312 | tf_op jit(solution)/shard_map/ppermute | solution.py:422
  42.5 2.5 %finish.6.refs_3_ = bf16[256,4096]{1,0:T(8,128)(2,1)} custom-call(f32[256,4096]{1,0:T(8,128)S(1)} %get-tuple-element.103.y_ref, f32[128,4096]{1,0:T(8,128)S(1)} %get-tuple-element.104.held_ref, f32[1,4096]{1,0:T(1,128)S(1)} %get-tuple-element.59.refs_2_.rate_ref, f32[16,4096]{1,0:T(8,128)S(1)} %get-tuple-element.60.refs_3_.wide_ref, ...), custom_call_target="tpu_custom_call" | custom-call | tf_op jit(solution)/shard_map/finish/pallas_call | solution.py:405
  45.1 0.6 %collective-permute-done.5 = f32[2,4096]{1,0:T(2,128)S(1)} collective-permute-done((f32[2,4096]{1,0:T(2,128)S(1)}, f32[2,4096]{1,0:T(2,128)S(1)}, u32[]{:S(2)}, u32[]{:S(2)}) %collective-permute-start.5) | collective-permute-done | bytes 32800 | tf_op jit(solution)/shard_map/ppermute | solution.py:422
  45.7 1.5 %collective-permute-start.6 = (f32[2,4096]{1,0:T(2,128)S(1)}, f32[2,4096]{1,0:T(2,128)S(1)}, u32[]{:S(2)}, u32[]{:S(2)}) collective-permute-start(f32[2,4096]{1,0:T(2,128)S(1)} %add.18), channel_id=1, source_target_pairs={{0,4},{2,6},{4,0},{6,2},{1,5},{3,7},{5,1},{7,3},{8,12},{10,14},{12... | collective-permute-start | bytes 98312 | tf_op jit(solution)/shard_map/ppermute | solution.py:422
  47.2 2.5 %finish.7 = bf16[256,4096]{1,0:T(8,128)(2,1)} custom-call(f32[256,4096]{1,0:T(8,128)S(1)} %get-tuple-element.103.y_ref, f32[128,4096]{1,0:T(8,128)S(1)} %get-tuple-element.104.held_ref, f32[1,4096]{1,0:T(1,128)S(1)} %get-tuple-element.59.refs_2_.rate_ref, f32[16,4096]{1,0:T(8,128)S(1)} %get-tuple-element.60.refs_3_.wide_ref, ...), custom_call_target="tpu_custom_call", output_to_operand_aliasing={{}: (8, {})} | custom-call | tf_op jit(solution)/shard_map/finish/pallas_call | solution.py:405
  49.8 1.2 %collective-permute-done.6 = f32[2,4096]{1,0:T(2,128)S(1)} collective-permute-done((f32[2,4096]{1,0:T(2,128)S(1)}, f32[2,4096]{1,0:T(2,128)S(1)}, u32[]{:S(2)}, u32[]{:S(2)}) %collective-permute-start.6) | collective-permute-done | bytes 32800 | tf_op jit(solution)/shard_map/ppermute | solution.py:422
  50.9 0.6 %fusion = (f32[1,4096]{1,0:T(1,128)}, f32[4096]{0:T(1024)S(1)}) fusion(f32[2,4096]{1,0:T(2,128)S(1)} %add.19), kind=kLoop, calls=%fused_computation.2 | loop fusion | bytes 65536 | tf_op jit(solution)/shard_map/slice | solution.py:434
  51.6 0.1 reshape_squeeze.3
  51.7 0.7 %copy.26 = f32[256,16]{0,1:T(8,128)} copy(f32[256,16]{1,0:T(8,128)S(1)} %reshape_squeeze.3) | data formatting | bytes 32768
  (4 shorter events, 0.1 us)
Async XLA Ops:
  0.6 0.7 %copy-start.1 = (f32[256,16]{0,1:T(8,128)S(1)}, f32[256,16]{0,1:T(8,128)}, u32[]{:S(2)}) copy-start(f32[256,16]{0,1:T(8,128)} %param.8) | copy-start | bytes 49156
  1.4 0.7 %copy-start.2 = (f32[256,16]{0,1:T(8,128)S(1)}, f32[256,16]{0,1:T(8,128)}, u32[]{:S(2)}) copy-start(f32[256,16]{0,1:T(8,128)} %param.7) | copy-start | bytes 49156
  2.1 8.9 %copy-start = (f32[4096]{0:T(1024)S(1)}, f32[4096]{0:T(1024)}, u32[]{:S(2)}) copy-start(f32[4096]{0:T(1024)} %param.9) | copy-start | bytes 49156
  7.9 9.4 %collective-permute-start = (f32[16,4096]{1,0:T(8,128)S(1)}, f32[16,4096]{1,0:T(8,128)S(1)}, u32[]{:S(2)}, u32[]{:S(2)}) collective-permute-start(f32[16,4096]{1,0:T(8,128)S(1)} %get-tuple-element.70.refs_6_), channel_id=1, source_target_pairs={{0,2},{2,0},{4,6},{6,4},{1,3},{3,1},{5,7},{7,5},{8,10},{10,8},{12,... | collective-permute-start | bytes 786440 | tf_op jit(solution)/shard_map/ppermute | solution.py:369
  17.4 6.6 %collective-permute-start.1 = (f32[16,4096]{1,0:T(8,128)S(1)}, f32[16,4096]{1,0:T(8,128)S(1)}, u32[]{:S(2)}, u32[]{:S(2)}) collective-permute-start(f32[16,4096]{1,0:T(8,128)S(1)} %multiply_add_fusion.refs_7_), channel_id=1, source_target_pairs={{2,4},{4,2},{3,5},{5,3},{10,12},{12,10},{11,13},{13,11},{18,20},{2... | collective-permute-start | bytes 786440 | tf_op jit(solution)/shard_map/ppermute | solution.py:369
  23.9 11.0 %collective-permute-start.2 = (f32[16,4096]{1,0:T(8,128)S(1)}, f32[16,4096]{1,0:T(8,128)S(1)}, u32[]{:S(2)}, u32[]{:S(2)}) collective-permute-start(f32[16,4096]{1,0:T(8,128)S(1)} %collective-permute-done.1.refs_1_.refs_8_), channel_id=1, source_target_pairs={{2,0},{4,6},{3,1},{5,7},{10,8},{12,14},{11,9},{13,15},{18,16},{20,... | collective-permute-start | bytes 786440 | tf_op jit(solution)/shard_map/ppermute | solution.py:369
  29.6 7.9 %collective-permute-start.3 = (f32[2,4096]{1,0:T(2,128)S(1)}, f32[2,4096]{1,0:T(2,128)S(1)}, u32[]{:S(2)}, u32[]{:S(2)}) collective-permute-start(f32[2,4096]{1,0:T(2,128)S(1)} %carry_grad.1), channel_id=1, source_target_pairs={{0,8},{8,0},{16,24},{24,16},{1,9},{9,1},{17,25},{25,17},{2,10},{10... | collective-permute-start | bytes 98312 | tf_op jit(solution)/shard_map/ppermute | solution.py:422
  37.5 4.2 %collective-permute-start.4 = (f32[2,4096]{1,0:T(2,128)S(1)}, f32[2,4096]{1,0:T(2,128)S(1)}, u32[]{:S(2)}, u32[]{:S(2)}) collective-permute-start(f32[2,4096]{1,0:T(2,128)S(1)} %add.16), channel_id=1, source_target_pairs={{0,16},{8,24},{16,0},{24,8},{1,17},{9,25},{17,1},{25,9},{2,18},{10... | collective-permute-start | bytes 98312 | tf_op jit(solution)/shard_map/ppermute | solution.py:422
  41.7 4.0 %collective-permute-start.5 = (f32[2,4096]{1,0:T(2,128)S(1)}, f32[2,4096]{1,0:T(2,128)S(1)}, u32[]{:S(2)}, u32[]{:S(2)}) collective-permute-start(f32[2,4096]{1,0:T(2,128)S(1)} %add.17), channel_id=1, source_target_pairs={{0,2},{2,0},{4,6},{6,4},{1,3},{3,1},{5,7},{7,5},{8,10},{10,8},{12,... | collective-permute-start | bytes 98312 | tf_op jit(solution)/shard_map/ppermute | solution.py:422
  45.7 5.2 %collective-permute-start.6 = (f32[2,4096]{1,0:T(2,128)S(1)}, f32[2,4096]{1,0:T(2,128)S(1)}, u32[]{:S(2)}, u32[]{:S(2)}) collective-permute-start(f32[2,4096]{1,0:T(2,128)S(1)} %add.18), channel_id=1, source_target_pairs={{0,4},{2,6},{4,0},{6,2},{1,5},{3,7},{5,1},{7,3},{8,12},{10,14},{12... | collective-permute-start | bytes 98312 | tf_op jit(solution)/shard_map/ppermute | solution.py:422
